TPU v7x, 256 devices: a whole 4x4x8 slice. The times are simulated.
256 devices in a mesh: seg: 8 (over y, core), ep: 32 (over z, x).
Axes of the slice: x: 4, y: 4, z: 8, core: 2. Of those that a mesh axis runs over, the one named last changes fastest.
Arguments:
- queries: bfloat16 [16384, 8192], P(('seg', 'ep')), may hold values from -6 to 6
- keys: bfloat16 [16384, 8192], P(('seg', 'ep')), may hold values from -1.25 to 1.25
- values: bfloat16 [16384, 8192], P(('seg', 'ep')), may hold values from -54 to 54
- log_decay: float32 [16384, 64], P('seg', 'ep'), may hold values from -1 to 0
- out_gain: float32 [8192], replicated, may hold values from 0.1 to 1.9
- out_proj: bfloat16 [8192, 6144], P('ep', 'seg'), may hold values from -0.0625 to 0.0625
- experts: int32 [2048, 2], P(('seg', 'ep')), may hold values from 0 to 15, all different within a row; in each aligned block of 8 rows (0 to 7, 8 to 15, ...) at most 2 rows name the same one
- gates: float32 [2048, 2], P(('seg', 'ep')), may hold values from 0.2 to 1
- up_weight: bfloat16 [32, 6144, 2304], P('ep', None, 'seg'), may hold values from -0.078125 to 0.078125
- down_weight: bfloat16 [32, 2304, 6144], P('ep', 'seg'), may hold values from -0.09375 to 0.09375
Outputs:
- attn_out: bfloat16 [16384, 8192], P(('seg', 'ep'))
- moe_out: bfloat16 [2048, 6144], P(('seg', 'ep'))
Inputs may be any that keep to these rules, and one draw needn't show every extreme that they name: Each row names two different experts. The 8 rows of one device name any one expert at most 2 times, and in some devices one expert exactly 2 times.
All inputs are finite; a program needn't handle non-finite values.
Results may differ from a plain program's by a relative error of at most 0.025.
Values may be sent and summed in bfloat16 or wider, within the bound.
No kernel may reach another device: no remote copies, remote signals or barrier semaphores. Data moves between devices by JAX's collectives and lax.ppermute only.
A program may use at most 128 MiB of HBM per device.

v0:
```python
import math

import jax
import jax.numpy as jnp
from jax import lax
from jax.sharding import Mesh
from jax.sharding import PartitionSpec as P

EP = ("ep_0", "ep_1")
SEG_EP = ("seg", "ep_0", "ep_1")


epsilon = 1e-06


def side_by_side(arrays, axis, dim, along):
    columns = [a.reshape(*a.shape[:along], -1) for a in arrays]
    both = jnp.concatenate(columns, axis=along)
    whole, at, done = (lax.all_gather(both, axis, axis=dim, tiled=True), 0, [])
    for a, column in zip(arrays, columns):
        section = whole[..., at : at + column.shape[along]]
        done.append(section.reshape(*section.shape[:along], *a.shape[along:]))
        at += column.shape[along]
    return tuple(done)


def sent_to_all(x, axis):
    devices = lax.axis_size(axis)
    return lax.all_to_all(jnp.broadcast_to(x[None], (devices, *x.shape)), axis, 0, 0, tiled=True)


def taken_together(x, axis):
    return sent_to_all(x, axis).sum(axis=0)


def scatter_axes(x, axes, dim):
    for axis in axes:
        x = lax.psum_scatter(x, axis, scatter_dimension=dim, tiled=True)
    return x


def route_tables(experts, gates, expert_count, capacity):
    token_count = experts.shape[0]
    flattened = experts.reshape(-1)
    onehot = (flattened[:, None] == jnp.arange(expert_count, dtype=jnp.int32)[None, :]).astype(
        jnp.int32
    )
    earlier = jnp.cumsum(onehot, axis=0) - onehot
    position = jnp.sum(earlier * onehot, axis=1)
    slot_index = (flattened * capacity + position).reshape(token_count, 2)
    columns = jnp.arange(expert_count * capacity, dtype=jnp.int32)
    matches = slot_index[:, :, None] == columns[None, None, :]
    dispatch = jnp.any(matches, axis=1).T.astype(jnp.bfloat16)
    combine = jnp.sum(jnp.where(matches, gates[:, :, None], 0.0), axis=1)
    return (dispatch, combine)


def expert_output(row_data, up_piece, down_piece):
    hidden = jax.nn.silu(jnp.dot(row_data, up_piece, preferred_element_type=jnp.float32)).astype(
        jnp.bfloat16
    )
    return jnp.dot(hidden, down_piece, preferred_element_type=jnp.float32)


def on_device(
    queries, keys, values, log_decay, out_gain, out_proj, experts, gates, up_weight, down_weight
):
    ep_count = lax.axis_size(EP)
    heads_local = log_decay.shape[1]
    head_dim = queries.shape[1] // (heads_local * ep_count)
    query_heads, key_heads, value_heads = (
        lax.all_to_all(queries, EP, split_axis=1, concat_axis=0, tiled=True),
        lax.all_to_all(keys, EP, split_axis=1, concat_axis=0, tiled=True),
        lax.all_to_all(values, EP, split_axis=1, concat_axis=0, tiled=True),
    )
    seg_length = query_heads.shape[0]
    query_heads = query_heads.reshape(seg_length, heads_local, head_dim)
    key_heads = key_heads.reshape(seg_length, heads_local, head_dim)
    value_heads = value_heads.reshape(seg_length, heads_local, head_dim)
    cumulative = jnp.cumsum(log_decay, axis=0)
    across = cumulative.T
    block_size = math.gcd(seg_length, 512)
    starts = jnp.arange(seg_length // block_size, dtype=jnp.int32) * block_size
    token_positions = jnp.arange(seg_length, dtype=jnp.int32)

    def block_mix(start):
        query_block = lax.dynamic_slice_in_dim(query_heads, start, block_size, 0)
        cum_block = lax.dynamic_slice_in_dim(across, start, block_size, 1)
        row_ids = start + jnp.arange(block_size, dtype=jnp.int32)
        causal = (row_ids[:, None] >= token_positions[None, :])[None]
        log_gap = cum_block[:, :, None] - across[:, None, :]
        weight = jnp.where(causal, jnp.exp(jnp.where(causal, log_gap, 0.0)), 0.0)
        scores = jnp.einsum(
            "thd,shd->hts", query_block, key_heads, preferred_element_type=jnp.float32
        )
        mixing = (scores * weight).astype(jnp.bfloat16)
        return jnp.einsum("hts,she->the", mixing, value_heads, preferred_element_type=jnp.float32)

    inside = lax.map(block_mix, starts).reshape(seg_length, heads_local, head_dim)
    ending = cumulative[-1]
    to_end = jnp.exp(ending[None, :] - cumulative)
    key_float = key_heads.astype(jnp.float32)
    value_float = value_heads.astype(jnp.float32)
    local_state = jnp.einsum("sh,shd,she->hde", to_end, key_float, value_float)
    all_ends, all_states = tuple(
        (
            part.astype(jnp.float32)
            for part in side_by_side(
                (ending[None].astype(jnp.bfloat16), local_state[None].astype(jnp.bfloat16)),
                "seg",
                0,
                2,
            )
        )
    )
    own_group = lax.axis_index("seg")
    group_ids = jnp.arange(all_ends.shape[0], dtype=jnp.int32)
    before = (group_ids < own_group)[:, None]
    through = jnp.cumsum(all_ends, axis=0)
    reaching = jnp.sum(jnp.where(before, all_ends, 0.0), axis=0)
    factors = jnp.where(before, jnp.exp(jnp.where(before, reaching[None, :] - through, 0.0)), 0.0)
    carried = jnp.einsum("gh,ghde->hde", factors, all_states)
    outside = jnp.exp(cumulative)[:, :, None] * jnp.einsum(
        "thd,hde->the", query_heads.astype(jnp.float32), carried
    )
    mixture = (inside + outside).astype(jnp.bfloat16).reshape(seg_length, heads_local * head_dim)
    token_mix = lax.all_to_all(mixture, EP, split_axis=0, concat_axis=1, tiled=True)
    as_float = token_mix.astype(jnp.float32)
    inv_rms = lax.rsqrt(jnp.mean(as_float * as_float, axis=1, keepdims=True) + epsilon)
    attn_out = (as_float * inv_rms * out_gain[None, :]).astype(jnp.bfloat16)
    row_stride = 8
    own_width = heads_local * head_dim
    feature_count = own_width * ep_count
    picked_float = mixture.reshape(seg_length // row_stride, row_stride, own_width)[:, 0].astype(
        jnp.float32
    )
    square_sums = taken_together(jnp.sum(picked_float * picked_float, axis=1), EP)
    picked_rms = lax.rsqrt(square_sums[:, None] / feature_count + epsilon)
    gain_slice = lax.dynamic_slice_in_dim(out_gain, lax.axis_index(EP) * own_width, own_width, 0)
    normed_rows = (picked_float * picked_rms * gain_slice[None, :]).astype(jnp.bfloat16)
    proj_terms = jnp.dot(
        normed_rows,
        lax.all_gather(out_proj, "seg", axis=1, tiled=True),
        preferred_element_type=jnp.float32,
    )
    moe_in = (
        scatter_axes(proj_terms.astype(jnp.bfloat16), EP, 0)
        .astype(jnp.float32)
        .astype(jnp.bfloat16)
    )
    expert_count = ep_count // 2
    token_count, model_width = moe_in.shape
    capacity = max(2, 4 * token_count // expert_count)
    dispatch, combine = route_tables(experts, gates, expert_count, capacity)
    up_piece = up_weight[0]
    down_piece = down_weight[0]
    slot_rows = jnp.dot(dispatch, moe_in, preferred_element_type=jnp.float32).astype(jnp.bfloat16)
    outgoing = jnp.repeat(slot_rows.reshape(expert_count, capacity, model_width), 2, axis=0)
    arrived = lax.all_to_all(outgoing, EP, split_axis=0, concat_axis=0, tiled=True).reshape(
        ep_count * capacity, model_width
    )
    gathered = lax.all_gather(arrived, "seg", axis=0, tiled=True)
    owned_sums = lax.psum_scatter(
        expert_output(gathered, up_piece, down_piece).astype(jnp.bfloat16),
        "seg",
        scatter_dimension=0,
        tiled=True,
    ).astype(jnp.float32)
    returned_back = lax.all_to_all(
        owned_sums.reshape(ep_count, capacity, model_width).astype(jnp.bfloat16),
        EP,
        split_axis=0,
        concat_axis=0,
        tiled=True,
    ).astype(jnp.float32)
    paired = returned_back.reshape(expert_count, 2, capacity, model_width)
    halves = (paired[:, 0] + paired[:, 1]).reshape(expert_count * capacity, model_width)
    summed = jnp.dot(combine, halves)
    moe_out = summed.astype(jnp.bfloat16)
    return (attn_out, moe_out)


def solution(mesh):
    torus = Mesh(mesh.devices.reshape(mesh.shape["seg"], 8, 4), ("seg", "ep_0", "ep_1"))
    placed = (
        P(SEG_EP, None),
        P(SEG_EP, None),
        P(SEG_EP, None),
        P("seg", EP),
        P(),
        P(EP, "seg"),
        P(SEG_EP, None),
        P(SEG_EP, None),
        P(EP, None, "seg"),
        P(EP, "seg", None),
    )
    return jax.shard_map(
        on_device,
        mesh=torus,
        in_specs=placed,
        out_specs=(P(SEG_EP, None), P(SEG_EP, None)),
        check_vma=False,
    )
```

profile of v0, /device:TPU:1, one launch (start us, length us, event | category | flops | bytes accessed | tf_op | source)
XLA Modules:
  0.0 518.4 jit_solution(4376102759249833830)
XLA Ops:
  9.7 12.1 %all-to-all-start.1 = ((bf16[64,32,256]{2,0,1:T(8,128)(2,1)}), bf16[64,32,256]{2,0,1:T(8,128)(2,1)}, u32[]{:S(2)}, u32[]{:S(2)}) async-start(bf16[64,32,256]{2,0,1:T(8,128)(2,1)} %bitcast.112), calls=%async_computation.1 | async-start | bytes 2097152 | tf_op jit(solution)/shard_map/all_to_all | solution.py:73
  24.1 23.9 %all-to-all-done.1 = bf16[64,32,256]{2,0,1:T(8,128)(2,1)} async-done(((bf16[64,32,256]{2,0,1:T(8,128)(2,1)}), bf16[64,32,256]{2,0,1:T(8,128)(2,1)}, u32[]{:S(2)}, u32[]{:S(2)}) %all-to-all-start.1) | async-done | bytes 1048608 | tf_op jit(solution)/shard_map/all_to_all | solution.py:73
  69.3 10.4 %all-to-all-done.2 = bf16[64,32,256]{2,0,1:T(8,128)(2,1)} async-done(((bf16[64,32,256]{2,0,1:T(8,128)(2,1)}), bf16[64,32,256]{2,0,1:T(8,128)(2,1)}, u32[]{:S(2)}, u32[]{:S(2)}) %all-to-all-start.2) | async-done | bytes 1048608 | tf_op jit(solution)/shard_map/all_to_all | solution.py:74
  79.7 7.0 %all-to-all-start = ((bf16[64,32,256]{2,0,1:T(8,128)(2,1)}), bf16[64,32,256]{2,0,1:T(8,128)(2,1)}, u32[]{:S(2)}, u32[]{:S(2)}) async-start(bf16[64,32,256]{2,0,1:T(8,128)(2,1)} %bitcast.111), calls=%async_computation | async-start | bytes 2097152 | tf_op jit(solution)/shard_map/all_to_all | solution.py:72
  99.5 16.1 %all_gather.9 = bf16[8,2,16385]{2,1,0:T(2,128)(2,1)S(1)} all-gather(bf16[1,2,16385]{2,1,0:T(2,128)(2,1)S(1)} %pad_maximum_fusion), channel_id=1, replica_groups=mesh['seg'=8,'ep_0'=8,'ep_1'=4] {'seg'}, dimensions={0}, use_global_device_ids=true | all-gather | bytes 589860 | tf_op jit(solution)/shard_map/all_gather | solution.py:19
  128.2 99.5 %while.11 = (s32[]{:T(128)}, f32[4,512,2,128]{1,0,3,2:T(4,128)}, s32[4]{0:T(128)S(1)}, bf16[2048,2,128]{2,0,1:T(8,128)(2,1)}, bf16[2048,2,128]{2,0,1:T(8,128)(2,...) while((s32[]{:T(128)}, f32[4,512,2,128]{1,0,3,2:T(4,128)}, ...), condition=%wide.region_3.4_spmd.clone, body=%wide.region_2.3_spmd.clone.sunk | while | flops 1085276672 | bytes 7110819 | solution.py:99
  133.4 6.6 %fusion.58 = f32[1,512,2,128]{3,1,2,0:T(8,128)} fusion(bf16[2048,2,128]{2,0,1:T(8,128)(2,1)} %get-tuple-element.204, bf16[2048,2,128]{2,0,1:T(8,128)(2,1)} %get-tuple-element.202, f32[2,2048]{1,0:T(2,128)} %get-tuple-element.203, f32[2,512]{1,0:T(2,128)S(1)} %constant_dynamic-slice_fusion.2, pred[512,2048]{1,0:T(8,128)(4,1)} %iota_compare_fusion.5, ...), kind=kOutput, calls=%fused_computation.4.clone.1 | convolution fusion | flops 1084227584 | bytes 3952644 | tf_op jit(solution)/shard_map/while/body/eval_jaxpr/hts,she->the/dot_general | solution.py:97
  141.9 11.1 %dynamic_update_slice.6 = f32[4,512,2,128]{1,0,3,2:T(4,128)} dynamic-update-slice(f32[4,512,2,128]{1,0,3,2:T(4,128)} %get-tuple-element.189, f32[1,512,2,128]{1,0,3,2:T(1,128)} %copy.204, s32[]{:T(128)} %get-tuple-element.188, s32[]{:T(128)} %constant.22.clone.1..sunk, s32[]{:T(128)} %constant.22.clone.1..sunk, s32[]{:T(128)} %constant.22.clone.1..sunk) | dynamic-update-slice | bytes 1048580 | tf_op jit(solution)/shard_map/while/body/jit(dynamic_update_index_in_dim)/dynamic_update_slice | solution.py:99
  158.3 6.6 %fusion.58 = f32[1,512,2,128]{3,1,2,0:T(8,128)} fusion(bf16[2048,2,128]{2,0,1:T(8,128)(2,1)} %get-tuple-element.204, bf16[2048,2,128]{2,0,1:T(8,128)(2,1)} %get-tuple-element.202, f32[2,2048]{1,0:T(2,128)} %get-tuple-element.203, f32[2,512]{1,0:T(2,128)S(1)} %constant_dynamic-slice_fusion.2, pred[512,2048]{1,0:T(8,128)(4,1)} %iota_compare_fusion.5, ...), kind=kOutput, calls=%fused_computation.4.clone.1 | convolution fusion | flops 1084227584 | bytes 3952644 | tf_op jit(solution)/shard_map/while/body/eval_jaxpr/hts,she->the/dot_general | solution.py:97
  166.8 11.1 %dynamic_update_slice.6 = f32[4,512,2,128]{1,0,3,2:T(4,128)} dynamic-update-slice(f32[4,512,2,128]{1,0,3,2:T(4,128)} %get-tuple-element.189, f32[1,512,2,128]{1,0,3,2:T(1,128)} %copy.204, s32[]{:T(128)} %get-tuple-element.188, s32[]{:T(128)} %constant.22.clone.1..sunk, s32[]{:T(128)} %constant.22.clone.1..sunk, s32[]{:T(128)} %constant.22.clone.1..sunk) | dynamic-update-slice | bytes 1048580 | tf_op jit(solution)/shard_map/while/body/jit(dynamic_update_index_in_dim)/dynamic_update_slice | solution.py:99
  183.2 6.6 %fusion.58 = f32[1,512,2,128]{3,1,2,0:T(8,128)} fusion(bf16[2048,2,128]{2,0,1:T(8,128)(2,1)} %get-tuple-element.204, bf16[2048,2,128]{2,0,1:T(8,128)(2,1)} %get-tuple-element.202, f32[2,2048]{1,0:T(2,128)} %get-tuple-element.203, f32[2,512]{1,0:T(2,128)S(1)} %constant_dynamic-slice_fusion.2, pred[512,2048]{1,0:T(8,128)(4,1)} %iota_compare_fusion.5, ...), kind=kOutput, calls=%fused_computation.4.clone.1 | convolution fusion | flops 1084227584 | bytes 3952644 | tf_op jit(solution)/shard_map/while/body/eval_jaxpr/hts,she->the/dot_general | solution.py:97
  191.7 11.1 %dynamic_update_slice.6 = f32[4,512,2,128]{1,0,3,2:T(4,128)} dynamic-update-slice(f32[4,512,2,128]{1,0,3,2:T(4,128)} %get-tuple-element.189, f32[1,512,2,128]{1,0,3,2:T(1,128)} %copy.204, s32[]{:T(128)} %get-tuple-element.188, s32[]{:T(128)} %constant.22.clone.1..sunk, s32[]{:T(128)} %constant.22.clone.1..sunk, s32[]{:T(128)} %constant.22.clone.1..sunk) | dynamic-update-slice | bytes 1048580 | tf_op jit(solution)/shard_map/while/body/jit(dynamic_update_index_in_dim)/dynamic_update_slice | solution.py:99
  216.5 11.1 %dynamic_update_slice.6 = f32[4,512,2,128]{1,0,3,2:T(4,128)} dynamic-update-slice(f32[4,512,2,128]{1,0,3,2:T(4,128)} %get-tuple-element.189, f32[1,512,2,128]{1,0,3,2:T(1,128)} %copy.204, s32[]{:T(128)} %get-tuple-element.188, s32[]{:T(128)} %constant.22.clone.1..sunk, s32[]{:T(128)} %constant.22.clone.1..sunk, s32[]{:T(128)} %constant.22.clone.1..sunk) | dynamic-update-slice | bytes 1048580 | tf_op jit(solution)/shard_map/while/body/jit(dynamic_update_index_in_dim)/dynamic_update_slice | solution.py:99
  246.7 9.5 %all-to-all-start.4 = ((f32[32,1,256]{2,1,0:T(1,128)}), f32[32,1,256]{2,1,0:T(1,128)}, u32[]{:S(2)}, u32[]{:S(2)}) async-start(f32[32,1,256]{2,1,0:T(1,128)} %broadcast_in_dim.85), calls=%async_computation.4 | async-start | bytes 65536 | tf_op jit(solution)/shard_map/all_to_all | solution.py:29
  257.1 7.9 %all-to-all-done.4 = f32[32,1,256]{2,1,0:T(1,128)} async-done(((f32[32,1,256]{2,1,0:T(1,128)}), f32[32,1,256]{2,1,0:T(1,128)}, u32[]{:S(2)}, u32[]{:S(2)}) %all-to-all-start.4) | async-done | bytes 32800 | tf_op jit(solution)/shard_map/all_to_all | solution.py:29
  270.7 39.1 %reduce-scatter.4.cloned.1.call-done = bf16[32,6144]{1,0:T(8,128)(2,1)} async-done(((bf16[256,6144]{1,0:T(8,128)(2,1)}), bf16[32,6144]{1,0:T(8,128)(2,1)}) %reduce-scatter.4.cloned.1.call-update) | async-done | bytes 393232 | tf_op jit(solution)/shard_map/reduce_scatter | solution.py:38
  313.2 22.4 %reduce-scatter.6.cloned.1.call-done = bf16[8,6144]{1,0:T(8,128)(2,1)} async-done(((bf16[32,6144]{1,0:T(8,128)(2,1)}), bf16[8,6144]{1,0:T(8,128)(2,1)}) %reduce-scatter.6.cloned.1.call-update) | async-done | bytes 98320 | tf_op jit(solution)/shard_map/reduce_scatter | solution.py:38
  341.0 27.1 %all_to_all.77 = bf16[32,2,6144]{2,1,0:T(2,128)(2,1)} all-to-all(bf16[32,2,6144]{2,1,0:T(2,128)(2,1)S(1)} %bitcast.113), channel_id=1, replica_groups=mesh['seg'=8,'ep_0'=8,'ep_1'=4] {'ep_0','ep_1'}, dimensions={0} | all-to-all | bytes 1572864 | tf_op jit(solution)/shard_map/all_to_all | solution.py:159
  371.2 44.6 %all-gather.5.cloned.1.call-done = bf16[512,6144]{1,0:T(8,128)(2,1)} async-done(((bf16[64,6144]{1,0:T(8,128)(2,1)}), bf16[512,6144]{1,0:T(8,128)(2,1)}) %all-gather.5.cloned.1.call-update) | async-done | bytes 6291472 | tf_op jit(solution)/shard_map/all_gather | solution.py:162
  415.8 12.0 %convolution_convert_fusion = bf16[512,6144]{1,0:T(8,128)(2,1)} fusion(bf16[1,288,6144]{2,1,0:T(8,128)(2,1)S(1)} %copy-done, bf16[512,6144]{1,0:T(8,128)(2,1)} %all-gather.5.cloned.1.call-done, bf16[1,6144,288]{1,2,0:T(8,128)(2,1)} %param.20), kind=kOutput, calls=%fused_computation.10 | convolution fusion | flops 3627761664 | bytes 19660800 | tf_op jit(solution)/shard_map/dot_general | solution.py:62
  430.4 9.7 %all-to-all-start.3 = ((bf16[32,64,256]{2,1,0:T(8,128)(2,1)}), bf16[32,64,256]{2,1,0:T(8,128)(2,1)}, u32[]{:S(2)}, u32[]{:S(2)}) async-start(bf16[32,64,256]{2,1,0:T(8,128)(2,1)} %all_to_all.65), calls=%async_computation.3 | async-start | bytes 2097152 | tf_op jit(solution)/shard_map/all_to_all | solution.py:127
  440.2 26.8 %all-to-all-done.3 = bf16[32,64,256]{2,1,0:T(8,128)(2,1)} async-done(((bf16[32,64,256]{2,1,0:T(8,128)(2,1)}), bf16[32,64,256]{2,1,0:T(8,128)(2,1)}, u32[]{:S(2)}, u32[]{:S(2)}) %all-to-all-start.3) | async-done | bytes 1048608 | tf_op jit(solution)/shard_map/all_to_all | solution.py:127
  475.0 9.7 %all-to-all-start.6 = ((bf16[32,2,6144]{2,1,0:T(2,128)(2,1)}), bf16[32,2,6144]{2,1,0:T(2,128)(2,1)}, u32[]{:S(2)}, u32[]{:S(2)}) async-start(bf16[32,2,6144]{2,1,0:T(2,128)(2,1)} %convert_element_type.93), calls=%async_computation.9 | async-start | bytes 1572864 | tf_op jit(solution)/shard_map/all_to_all | solution.py:169
  487.5 17.6 %all-to-all-done.6 = bf16[32,2,6144]{2,1,0:T(2,128)(2,1)} async-done(((bf16[32,2,6144]{2,1,0:T(2,128)(2,1)}), bf16[32,2,6144]{2,1,0:T(2,128)(2,1)}, u32[]{:S(2)}, u32[]{:S(2)}) %all-to-all-start.6) | async-done | bytes 786464 | tf_op jit(solution)/shard_map/all_to_all | solution.py:169
  (122 shorter events, 137.7 us)
Async XLA Ops:
  7.2 408.6 %copy-start = (bf16[1,288,6144]{2,1,0:T(8,128)(2,1)S(1)}, bf16[1,288,6144]{2,1,0:T(8,128)(2,1)}, u32[]{:S(2)}) copy-start(bf16[1,288,6144]{2,1,0:T(8,128)(2,1)} %param.21) | copy-start | bytes 10616836
  9.7 45.6 %copy-start.4 = (f32[2048,2]{0,1:T(2,128)S(1)}, f32[2048,2]{0,1:T(2,128)}, u32[]{:S(2)}) copy-start(f32[2048,2]{0,1:T(2,128)} %param.15) | copy-start | bytes 49156
  9.7 38.3 %all-to-all-start.1 = ((bf16[64,32,256]{2,0,1:T(8,128)(2,1)}), bf16[64,32,256]{2,0,1:T(8,128)(2,1)}, u32[]{:S(2)}, u32[]{:S(2)}) async-start(bf16[64,32,256]{2,0,1:T(8,128)(2,1)} %bitcast.112), calls=%async_computation.1 | async-start | bytes 2097152 | tf_op jit(solution)/shard_map/all_to_all | solution.py:73
  48.0 31.8 %all-to-all-start.2 = ((bf16[64,32,256]{2,0,1:T(8,128)(2,1)}), bf16[64,32,256]{2,0,1:T(8,128)(2,1)}, u32[]{:S(2)}, u32[]{:S(2)}) async-start(bf16[64,32,256]{2,0,1:T(8,128)(2,1)} %bitcast.110), calls=%async_computation.2 | async-start | bytes 2097152 | tf_op jit(solution)/shard_map/all_to_all | solution.py:74
  54.5 211.4 %all-gather.3.cloned.1.call-start = ((), (), s32[]{:S(2)}) async-start(), calls=%async_computation.10 | async-start | bytes 3538944 | tf_op jit(solution)/shard_map/all_gather | solution.py:143
  79.7 44.0 %all-to-all-start = ((bf16[64,32,256]{2,0,1:T(8,128)(2,1)}), bf16[64,32,256]{2,0,1:T(8,128)(2,1)}, u32[]{:S(2)}, u32[]{:S(2)}) async-start(bf16[64,32,256]{2,0,1:T(8,128)(2,1)} %bitcast.111), calls=%async_computation | async-start | bytes 2097152 | tf_op jit(solution)/shard_map/all_to_all | solution.py:72
  98.5 21.0 %copy-start.1 = (bf16[2048,2,128]{2,1,0:T(2,128)(2,1)S(1)}, bf16[2048,2,128]{2,1,0:T(2,128)(2,1)}, u32[]{:S(2)}) copy-start(bf16[2048,2,128]{2,1,0:T(2,128)(2,1)} %reshape.159) | copy-start | bytes 3145732
  120.7 7.4 %copy-start.7 = (bf16[8,2,1]{0,1,2:T(2,128)(2,1)}, bf16[8,2,1]{0,1,2:T(2,128)(2,1)S(1)}, u32[]{:S(2)}) copy-start(bf16[8,2,1]{0,1,2:T(2,128)(2,1)S(1)} %copy.159) | copy-start | bytes 100
  227.6 6.7 %copy-start.3 = (f32[2048,2]{0,1:T(2,128)S(1)}, f32[2048,2]{0,1:T(2,128)}, u32[]{:S(2)}) copy-start(f32[2048,2]{0,1:T(2,128)} %get-tuple-element.131) | copy-start | bytes 49156
  245.3 0.7 copy-start.2
  246.7 18.3 %all-to-all-start.4 = ((f32[32,1,256]{2,1,0:T(1,128)}), f32[32,1,256]{2,1,0:T(1,128)}, u32[]{:S(2)}, u32[]{:S(2)}) async-start(f32[32,1,256]{2,1,0:T(1,128)} %broadcast_in_dim.85), calls=%async_computation.4 | async-start | bytes 65536 | tf_op jit(solution)/shard_map/all_to_all | solution.py:29
  256.3 53.5 %reduce-scatter.4.cloned.1.call-start = ((), (), s32[]{:S(2)}) async-start(), calls=%async_computation.11 | async-start | bytes 3538944 | tf_op jit(solution)/shard_map/reduce_scatter | solution.py:38
  270.6 39.4 %copy-start.5 = (s32[8,2]{0,1:T(2,128)S(1)}, s32[8,2]{0,1:T(2,128)}, u32[]{:S(2)}) copy-start(s32[8,2]{0,1:T(2,128)} %param.18) | copy-start | bytes 196
  270.6 65.0 %reduce-scatter.6.cloned.1.call-start = ((), (), s32[]{:S(2)}) async-start(), calls=%async_computation.12 | async-start | bytes 491520 | tf_op jit(solution)/shard_map/reduce_scatter | solution.py:38
  309.8 106.0 %all-gather.5.cloned.1.call-start = ((), (), s32[]{:S(2)}) async-start(), calls=%async_computation.13 | async-start | bytes 7077888 | tf_op jit(solution)/shard_map/all_gather | solution.py:162
  371.1 101.0 %reduce-scatter.8.cloned.1.call-start = ((), (), s32[]{:S(2)}) async-start(), calls=%async_computation.14 | async-start | bytes 7077888 | tf_op jit(solution)/shard_map/reduce_scatter | solution.py:163
  427.8 12.2 %copy-start.6 = (f32[8,2]{0,1:T(2,128)S(1)}, f32[8,2]{0,1:T(2,128)}, u32[]{:S(2)}) copy-start(f32[8,2]{0,1:T(2,128)} %param.19) | copy-start | bytes 196
  430.4 36.5 %all-to-all-start.3 = ((bf16[32,64,256]{2,1,0:T(8,128)(2,1)}), bf16[32,64,256]{2,1,0:T(8,128)(2,1)}, u32[]{:S(2)}, u32[]{:S(2)}) async-start(bf16[32,64,256]{2,1,0:T(8,128)(2,1)} %all_to_all.65), calls=%async_computation.3 | async-start | bytes 2097152 | tf_op jit(solution)/shard_map/all_to_all | solution.py:127
  475.0 30.1 %all-to-all-start.6 = ((bf16[32,2,6144]{2,1,0:T(2,128)(2,1)}), bf16[32,2,6144]{2,1,0:T(2,128)(2,1)}, u32[]{:S(2)}, u32[]{:S(2)}) async-start(bf16[32,2,6144]{2,1,0:T(2,128)(2,1)} %convert_element_type.93), calls=%async_computation.9 | async-start | bytes 1572864 | tf_op jit(solution)/shard_map/all_to_all | solution.py:169
Sparse Core Ops, SparseCore 0:
  57.1 33.4 all-gather.2
  270.8 38.9 reduce-scatter.3
  312.3 23.2 reduce-scatter.5
  371.2 44.5 all-gather.4
  428.0 44.1 reduce-scatter.7
where the time goes:
time: 524 us; the launch traced here: 518 us
  waiting for transfers between devices  194 us (37%)
  local copies, waits for them, and re-layouts  115 us (22%)
  starting transfers between devices  54.8 us (10%)
  matrix products  54.1 us (10%)
  blocking collectives  43.2 us (8%)
  other arithmetic  36.2 us (7%)
  between operations  14 us (3%)
  loops' own time  6.62 us (1%)
    reduce_scatter x2, waiting for transfers between devices, scatter_axes(): x = lax.psum_scatter(x, axis, scatter_dimension=dim, tiled=True)  61.5 us
    dynamic_update_slice x8, local copies, waits for them, and re-layouts, on_device(): lax.map(block_mix, starts).reshape(seg_length, heads_local, head_dim)  52.2 us
    all_gather x1, waiting for transfers between devices, on_device(): gathered = lax.all_gather(arrived, 'seg', axis=0, tiled=True)  44.6 us
    all_to_all x1, blocking collectives, on_device(): lax.all_to_all(outgoing, EP, split_axis=0, concat_axis=0, tiled=True)  27.1 us
    all_to_all x1, waiting for transfers between devices, on_device(): lax.all_to_all(mixture, EP, split_axis=0, concat_axis=1, tiled=True)  26.8 us
    dot_general x4, matrix products, block_mix(): jnp.einsum('hts,she->the', mixing, value_heads, preferred_element_type=jn...  26.3 us
    all_to_all x1, waiting for transfers between devices, on_device(): lax.all_to_all(keys, EP, split_axis=1, concat_axis=0, tiled=True)  23.9 us
    all_to_all x1, waiting for transfers between devices, on_device(): lax.all_to_all(owned_sums.reshape(ep_count, capacity, model_width).astype...  17.6 us
  transfers between devices with their start and end apart: 11, of which 9 were waited for; matrix products, arithmetic and copies ran while one was open for 32% of the time, Pallas kernels for 0%

commit v1 on v0

v1 whole, which is shorter than its diff:
```python
import jax
import jax.numpy as jnp
from jax import lax
from jax.experimental import pallas as pl
from jax.experimental.pallas import tpu as pltpu
from jax.sharding import Mesh
from jax.sharding import PartitionSpec as P

SEG = ("y", "c")
EP = ("z", "x")
SEG_EP = SEG + EP

HEAD = 128
PAIR = 2 * HEAD
EPS = 1e-06
bf16 = jnp.bfloat16
f32 = jnp.float32


def shifted(v, axis, by):
    n = lax.axis_size(axis)
    return lax.ppermute(v, axis, [(i, (i + by) % n) for i in range(n)])


def kernel_call(body, outs, args, scalars=0, flops=0, steps=None, blocks=None):
    moved = sum(a.size * a.dtype.itemsize for a in list(args) + list(outs))
    tables = [pl.BlockSpec(memory_space=pltpu.SMEM) for _ in range(scalars)]
    arrays = list(args[scalars:]) + list(outs)
    if steps is None:
        specs = [pl.BlockSpec(memory_space=pltpu.VMEM) for _ in arrays]
    else:
        specs = []
        for a, dim in zip(arrays, blocks):
            shape = tuple(n // steps if i == dim else n for i, n in enumerate(a.shape))
            index = lambda i, dim=dim, rank=len(shape): tuple(i if j == dim else 0 for j in range(rank))
            specs.append(pl.BlockSpec(shape, index))
    inputs = len(args) - scalars
    if steps is not None:
        args = [
            pltpu.with_memory_space_constraint(a, pltpu.HBM)
            if i >= scalars and a.size * a.dtype.itemsize >= 1 << 18
            else a
            for i, a in enumerate(args)
        ]
    return pl.pallas_call(
        body,
        out_shape=tuple(outs),
        grid=() if steps is None else (steps,),
        in_specs=tables + specs[:inputs],
        out_specs=tuple(specs[inputs:]),
        compiler_params=pltpu.CompilerParams(vmem_limit_bytes=2 * moved + (8 << 20)),
        cost_estimate=pl.CostEstimate(flops=flops, transcendentals=0, bytes_accessed=moved),
    )(*args)


def struct(shape, dtype):
    return jax.ShapeDtypeStruct(shape, dtype)


def dot(a, b, dims):
    return lax.dot_general(a, b, (dims, ((), ())), preferred_element_type=f32)


def pack_pair_body(ids, k, v, *outs):
    groups = k.shape[1] // (4 * PAIR)
    for d in range(4):
        at = lax.rem(ids[0] + d, 4) * PAIR
        for g in range(groups):
            cols = pl.ds(pl.multiple_of(at + g * 4 * PAIR, PAIR), PAIR)
            outs[d][0, :, g * PAIR : (g + 1) * PAIR] = k[:, cols]
            outs[d][1, :, g * PAIR : (g + 1) * PAIR] = v[:, cols]


def pack_body(ids, q, *outs):
    groups = q.shape[1] // (4 * PAIR)
    for d in range(4):
        at = lax.rem(ids[0] + d, 4) * PAIR
        for g in range(groups):
            cols = pl.ds(pl.multiple_of(at + g * 4 * PAIR, PAIR), PAIR)
            outs[d][:, g * PAIR : (g + 1) * PAIR] = q[:, cols]


def queries_of(pieces, h):
    return jnp.concatenate([p[:, h * HEAD : (h + 1) * HEAD] for p in pieces], axis=0)


def rows_of(pieces, lead, h):
    cols = slice(h * HEAD, (h + 1) * HEAD)
    return jnp.concatenate([p[lead, :, cols] for p in pieces], axis=0)


def chunk_state_body(kv0, kv1, kv2, kv3, rel_col, tot_row, out):
    pieces = (kv0, kv1, kv2, kv3)
    to_end = jnp.exp(tot_row[0] - rel_col[0])
    for h in range(rel_col.shape[2]):
        k = rows_of(pieces, 0, h).astype(f32)
        weighted = (k * to_end[:, h : h + 1]).astype(bf16)
        state = dot(weighted, rows_of(pieces, 1, h), ((0,), (0,)))
        out[h // 2, (h % 2) * HEAD : (h % 2 + 1) * HEAD, :] = state.astype(bf16)


def inside_body(ids, q0, q1, q2, q3, kv0, kv1, kv2, kv3, rel_col, rel_row, out):
    qs, kvs = (q0, q1, q2, q3), (kv0, kv1, kv2, kv3)
    length, block = rel_col.shape[1], q0.shape[0]

    def positions(axis):
        i = lax.broadcasted_iota(jnp.int32, (length, length), axis)
        return ((ids[0] + 4 - i // block) & 3) * block + (i & (block - 1))

    causal = positions(0) >= positions(1)
    for h in range(rel_col.shape[2]):
        gap = rel_col[0, :, h : h + 1] - rel_row[0, h : h + 1, :]
        weight = jnp.exp(jnp.where(causal, gap, -jnp.inf))
        scores = dot(queries_of(qs, h), rows_of(kvs, 0, h), ((1,), (1,)))
        mixing = (scores * weight).astype(bf16)
        out[:, h * HEAD : (h + 1) * HEAD] = dot(mixing, rows_of(kvs, 1, h), ((1,), (0,)))


def group_state_body(dec, s, info, out):
    for h in range(2):
        rows = slice(h * HEAD, (h + 1) * HEAD)
        total = s[0, rows, :].astype(f32)
        for z in range(1, s.shape[0]):
            total = total * dec[h, z] + s[z, rows, :].astype(f32)
        out[rows, :] = total.astype(bf16)
    out[PAIR:, :] = info[...]


def prefix_body(ids, dec, s, g0, g1, out):
    own = ids[1] * 2 + ids[2]
    each = g0.shape[0] // 4
    slots = [(g, d * each, r) for r, g in enumerate((g0, g1)) for d in range(4)]
    group = [
        lax.rem(ids[1] + 4 - d, 4) * 2 + ((ids[2] + r) & 1) for r in range(2) for d in range(4)
    ]
    for h in range(2):
        rows = slice(h * HEAD, (h + 1) * HEAD)

        def ending(slot):
            g, at, _ = slots[slot]
            first = at + PAIR + 8 + 3 * h
            e = [g[first + k : first + k + 1, :].astype(f32) for k in range(3)]
            return (e[0] + e[1]) + e[2]

        ends = [ending(slot) for slot in range(8)]
        state = jnp.zeros((HEAD, HEAD), f32)
        for i, (g, at, _) in enumerate(slots):
            gap = jnp.zeros((1, HEAD), f32)
            for j in range(8):
                between = (group[i] < group[j]) & (group[j] < own)
                gap = gap + jnp.where(between, 1.0, 0.0) * ends[j]
            factor = jnp.where(group[i] < own, 1.0, 0.0) * jnp.exp(gap)
            state = state + factor * g[at + h * HEAD : at + (h + 1) * HEAD, :].astype(f32)
        for z in range(s.shape[0]):
            out[z, rows, :] = state.astype(bf16)
            state = state * dec[h, z] + s[z, rows, :].astype(f32)


def mix_body(inside, q0, q1, q2, q3, prefix, rel_col, gain, m0, m1, m2, m3, rows_out, squares):
    qs, outs = (q0, q1, q2, q3), (m0, m1, m2, m3)
    length, block = rel_col.shape[1], q0.shape[0]
    picked = length // 8
    step, steps = pl.program_id(0), pl.num_programs(0)
    width = inside.shape[1]
    from_start = jnp.exp(rel_col[0])
    row = lax.broadcasted_iota(jnp.int32, (picked, length), 0)
    col = lax.broadcasted_iota(jnp.int32, (picked, length), 1)
    pick = (col == row * 8).astype(f32).astype(bf16)

    @pl.when(step == 0)
    def _():
        squares[...] = jnp.zeros_like(squares)

    for h in range(rel_col.shape[2]):
        cols = slice(h * HEAD, (h + 1) * HEAD)
        outside = dot(
            queries_of(qs, h),
            prefix[h // 2, (h % 2) * HEAD : (h % 2 + 1) * HEAD, :],
            ((1,), (0,)),
        )
        mixed = (inside[:, cols] + from_start[:, h : h + 1] * outside).astype(bf16)
        for d in range(4):
            outs[d][:, cols] = mixed[d * block : (d + 1) * block]
        rows = dot(pick, mixed, ((1,), (0,)))
        squares[...] += rows * rows
        at = pl.multiple_of(step * width + h * HEAD, HEAD)
        rows_out[:, pl.ds(at, HEAD)] = (rows * gain[:, cols]).astype(bf16)

    @pl.when(step == steps - 1)
    def _():
        total = jnp.sum(squares[...], axis=1, keepdims=True)
        high = total.astype(bf16).astype(f32)
        lane = lax.broadcasted_iota(jnp.int32, (picked, HEAD), 1)
        extra = jnp.where(lane == 0, high, jnp.where(lane == 1, total - high, 0.0))
        rows_out[:, rows_out.shape[1] - HEAD :] = extra.astype(bf16)


def project_body(r0, r1, weight, p0, p1, p2, p3):
    outs = (p0, p1, p2, p3)
    features, width = weight.shape
    for half, r in enumerate((r0, r1)):
        terms = dot(r[:, :features], weight[...], ((1,), (0,)))
        terms = terms.reshape(4, 4, 8, width)
        extra = r[:, features:].astype(f32).reshape(4, 4, 8, HEAD)
        for d in range(4):
            at = slice(half * 32, (half + 1) * 32)
            outs[d][at, :width] = terms[:, d].reshape(32, width).astype(bf16)
            outs[d][at, width:] = extra[:, d].reshape(32, HEAD).astype(bf16)


def dispatch_body(p0, p1, p2, p3, slots, out, *, features):
    width = out.shape[2]
    total = (p0[...].astype(f32) + p1[...].astype(f32)) + (p2[...].astype(f32) + p3[...].astype(f32))
    squares = total[:, width : width + 1] + total[:, width + 1 : width + 2]
    scale = lax.rsqrt(squares * (1.0 / features) + EPS)
    moe_in = (total[:, :width] * scale).astype(bf16)
    per = out.shape[1]
    count = (out.shape[0] // 2) * per
    target = lax.broadcasted_iota(jnp.int32, (count, total.shape[0]), 0)
    chosen = (target == slots[0:1, :]) | (target == slots[1:2, :])
    sent = dot(chosen.astype(f32).astype(bf16), moe_in, ((1,), (0,))).astype(bf16)
    for e in range(out.shape[0] // 2):
        block = sent[e * per : (e + 1) * per]
        out[2 * e] = block
        out[2 * e + 1] = block


def up_body(ids, own, other, w0, w1, w2, w3, *outs):
    width = own.shape[1]
    mine = pl.ds(pl.multiple_of(ids[2] * width, HEAD), width)
    rest = pl.ds(pl.multiple_of((1 - ids[2]) * width, HEAD), width)
    for w, out in zip((w0, w1, w2, w3), outs):
        part = dot(w[:, mine], own[...], ((1,), (1,)))
        part = part + dot(w[:, rest], other[...], ((1,), (1,)))
        out[...] = part.astype(bf16)


def down_body(ids, h0, h1, h2, h3, w0, w1, w2, w3, keep, send):
    width = keep.shape[1]
    mine = pl.ds(pl.multiple_of(ids[2] * width, HEAD), width)
    rest = pl.ds(pl.multiple_of((1 - ids[2]) * width, HEAD), width)
    hs, ws = (h0, h1, h2, h3), (w0, w1, w2, w3)
    send[...] = sum(dot(h[...], w[:, rest], ((0,), (0,))) for h, w in zip(hs, ws)).astype(bf16)
    keep[...] = sum(dot(h[...], w[:, mine], ((0,), (0,))) for h, w in zip(hs, ws))


def combine_body(ids, back, table, out):
    count = back.shape[0]
    lane = lax.broadcasted_iota(jnp.int32, (table.shape[0], count), 1)
    slot = ((lane >> 5) * 16 + (lane & 15)).astype(f32)
    gate = jnp.where(slot == table[:, 0:1], table[:, 2:3], 0.0) + jnp.where(
        slot == table[:, 1:2], table[:, 3:4], 0.0
    )
    high = gate.astype(bf16)
    low = (gate - high.astype(f32)).astype(bf16)
    total = dot(high, back[...], ((1,), (0,))) + dot(low, back[...], ((1,), (0,)))
    for r in range(2):
        for d in range(4):
            seg = lax.rem(ids[1] + 4 - d, 4) * 2 + ((ids[2] + r) & 1)
            at = (r * 4 + d) * 8
            out[seg] = total[at : at + 8].astype(bf16)


def norm_body(ids, m0, m1, m2, m3, gain, out):
    pieces = (m0, m1, m2, m3)
    width = m0.shape[1]
    total = jnp.zeros((m0.shape[0], 1), f32)
    for m in pieces:
        as_float = m[...].astype(f32)
        total = total + jnp.sum(as_float * as_float, axis=1, keepdims=True)
    scale = lax.rsqrt(total * (1.0 / (4 * width)) + EPS)
    for d, m in enumerate(pieces):
        at = lax.rem(ids[0] + d, 4) * PAIR
        for g in range(width // PAIR):
            cols = pl.ds(pl.multiple_of(at + g * 4 * PAIR, PAIR), PAIR)
            values = m[:, g * PAIR : (g + 1) * PAIR].astype(f32)
            out[:, cols] = (values * scale * gain[:, cols]).astype(bf16)


def over_seg(v):
    mine = jnp.concatenate([v] + [shifted(v, "y", d) for d in range(1, 4)], axis=0)
    return mine, shifted(mine, "c", 1)


def in_three(v):
    high = lax.reduce_precision(v, 8, 7)
    middle = lax.reduce_precision(v - high, 8, 7)
    return high, middle, lax.reduce_precision(v - high - middle, 8, 7)


def slot_ids(experts, expert_count):
    flat = experts.reshape(-1)
    onehot = (flat[:, None] == jnp.arange(expert_count, dtype=jnp.int32)[None, :]).astype(jnp.int32)
    earlier = flat[:, None] == flat[None, :]
    before = jnp.arange(flat.size)[:, None] > jnp.arange(flat.size)[None, :]
    position = jnp.sum((earlier & before).astype(jnp.int32), axis=1)
    return flat.reshape(experts.shape), position.reshape(experts.shape)


def on_device(
    queries, keys, values, log_decay, out_gain, out_proj, experts, gates, up_weight, down_weight
):
    x, y, c = lax.axis_index("x"), lax.axis_index("y"), lax.axis_index("c")
    ids = jnp.stack([x, y, c]).astype(jnp.int32)
    tokens, all_features = queries.shape
    features = all_features // 4
    heads = features // HEAD
    length = 4 * tokens
    n_z = lax.axis_size("z")
    model_slice = out_proj.shape[1]
    rows_dev = experts.shape[0]
    expert_count = 4 * n_z // 2

    kv_out = kernel_call(
        pack_pair_body, [struct((2, tokens, features), bf16)] * 4, (ids, keys, values), scalars=1
    )
    kv_out = list(kv_out)
    kv = [None] + [shifted(kv_out[d], "x", d) for d in range(1, 4)]
    queries, kv[1] = lax.optimization_barrier((queries, kv[1]))
    q_out = kernel_call(pack_body, [struct((tokens, features), bf16)] * 4, (ids, queries), scalars=1)
    q = [q_out[0]] + [shifted(q_out[d], "x", d) for d in range(1, 4)]

    weight_out = lax.all_gather(out_proj, "z", axis=0, tiled=True)

    def sliced(w):
        quarter = w.shape[1] // 4
        return [
            lax.dynamic_slice_in_dim(w, ((y + d) % 4) * quarter, quarter, 1) for d in range(4)
        ]

    def over_y(pieces):
        return [pieces[0]] + [shifted(pieces[d], "y", d) for d in range(1, 4)]

    up = sliced(up_weight[0].T)
    kv[0], log_decay, *up = lax.optimization_barrier((kv_out[0], log_decay, *up))
    up = over_y(up)

    decay = log_decay.T.reshape(2 * n_z, length)
    upto = (
        jnp.arange(length, dtype=jnp.int32)[:, None] <= jnp.arange(length, dtype=jnp.int32)[None, :]
    ).astype(f32)
    rel_own = jnp.dot(decay, upto, precision=lax.Precision.HIGHEST).reshape(2, n_z, length)
    chunk_total = rel_own[:, :, -1]
    chunk_decay = jnp.exp(chunk_total)
    rel = lax.all_to_all(rel_own.transpose(1, 0, 2), "z", 0, 0, tiled=True).reshape(heads, length)
    by_source = rel.reshape(heads, 4, tokens)
    order = (x + 4 - jnp.arange(4, dtype=jnp.int32)) % 4
    rel_row = jnp.concatenate(
        [lax.dynamic_index_in_dim(by_source, order[d], 1, keepdims=False) for d in range(4)], axis=1
    )
    steps = 4
    rel_row = rel_row.reshape(steps, heads // steps, length)
    rel_col = rel_row.transpose(0, 2, 1)
    tot_row = rel[:, -1].reshape(steps, 1, heads // steps)

    expert, position = slot_ids(experts, expert_count)
    group_total = jnp.repeat(jnp.stack(in_three(jnp.sum(chunk_total, axis=1)), 1).reshape(6, 1), 128, 1)
    columns = [expert.astype(f32), position.astype(f32), *in_three(gates)]
    info = jnp.concatenate(columns + [jnp.zeros((rows_dev, 128 - 2 * len(columns)), f32)], axis=1)
    info = jnp.concatenate([info, group_total, jnp.zeros((2, 128), f32)], axis=0).astype(bf16)

    states = kernel_call(
        chunk_state_body,
        [struct((n_z, PAIR, HEAD), bf16)],
        (*kv, rel_col, tot_row),
        flops=2 * length * features * HEAD,
        steps=steps,
        blocks=(2, 2, 2, 2, 0, 0, 0),
    )[0]
    states, weight_out, *down = lax.optimization_barrier(
        (states, weight_out, *sliced(down_weight[0]))
    )
    down = over_y(down)
    states = lax.all_to_all(states, "z", 0, 0, tiled=True)
    inside = kernel_call(
        inside_body,
        [struct((length, features), f32)],
        (ids, *q, *kv, rel_col, rel_row),
        scalars=1,
        flops=4 * length * length * features,
        steps=steps,
        blocks=(1,) * 4 + (2,) * 4 + (0, 0, 1),
    )[0]
    states, *up = lax.optimization_barrier((states, *up))
    local = kernel_call(
        group_state_body, [struct((PAIR + 16, HEAD), bf16)], (chunk_decay, states, info), scalars=1
    )[0]
    *groups, down[2] = lax.optimization_barrier((*over_seg(local), down[2]))
    prefix = kernel_call(
        prefix_body,
        [struct((n_z, PAIR, HEAD), bf16)],
        (ids, chunk_decay, states, *groups),
        scalars=2,
    )[0]
    prefix = lax.all_to_all(prefix, "z", 0, 0, tiled=True)
    info = jnp.concatenate(
        [g.reshape(4, PAIR + 16, HEAD)[:, PAIR : PAIR + rows_dev] for g in groups], axis=0
    ).astype(f32)
    slot = jnp.arange(8, dtype=jnp.int32)
    group = ((y + 4 - slot % 4) % 4) * 2 + (c + slot // 4) % 2
    slots = info[..., 0:2] * 16.0 + group[:, None, None].astype(f32) * 2.0 + info[..., 2:4]
    slots = slots.reshape(8 * rows_dev, 2)
    gate = (info[..., 4:6] + info[..., 6:8] + info[..., 8:10]).reshape(8 * rows_dev, 2)
    slot_rows = slots.T.astype(jnp.int32)
    combine_table = jnp.concatenate([slots, gate, jnp.zeros((8 * rows_dev, 124), f32)], axis=1)
    gain_own = lax.dynamic_index_in_dim(
        out_gain.reshape(n_z, 4, PAIR), x, 1, keepdims=False
    ).reshape(1, features)
    *mixed, rows, _ = kernel_call(
        mix_body,
        [struct((tokens, features), bf16)] * 4
        + [struct((length // 8, features + HEAD), bf16), struct((length // 8, HEAD), f32)],
        (inside, *q, prefix, rel_col, gain_own),
        flops=2 * length * features * HEAD,
        steps=steps,
        blocks=(1,) * 5 + (0, 0, 1) + (1,) * 4 + (None, None),
    )

    terms = kernel_call(
        project_body,
        [struct((8 * rows_dev, model_slice + HEAD), bf16)] * 4,
        (*over_seg(rows), weight_out),
        flops=2 * length * features * model_slice,
    )
    terms = [terms[0]] + [shifted(terms[d], "x", -d) for d in range(1, 4)]
    outgoing = kernel_call(
        lambda *refs: dispatch_body(*refs, features=all_features),
        [struct((2 * expert_count, 16, model_slice), bf16)],
        (*terms, slot_rows),
    )[0]
    arrived = lax.all_to_all(outgoing, EP, 0, 0, tiled=True).reshape(-1, model_slice)
    arrived, down[1], down[3], combine_table = lax.optimization_barrier(
        (arrived, down[1], down[3], combine_table)
    )

    hidden_dev = up[0].shape[0]
    parts = kernel_call(
        up_body,
        [struct((hidden_dev, arrived.shape[0]), bf16)] * 4,
        (ids, arrived, shifted(arrived, "c", 1), *up),
        scalars=1,
        flops=16 * arrived.size * hidden_dev,
    )
    parts = [parts[0]] + [shifted(parts[d], "y", -d) for d in range(1, 4)]
    hidden = jax.nn.silu(sum(p.astype(f32) for p in parts)).astype(bf16)
    mixed = [mixed[0]] + [shifted(mixed[d], "x", -d) for d in range(1, 4)]
    hiddens = [hidden] + [shifted(hidden, "y", d) for d in range(1, 4)]
    keep, send = kernel_call(
        down_body,
        [struct(arrived.shape, f32), struct(arrived.shape, bf16)],
        (ids, *hiddens, *down),
        scalars=1,
        flops=16 * arrived.size * hidden_dev,
    )
    result = (keep + shifted(send, "c", 1).astype(f32)).astype(bf16)
    back = lax.all_to_all(
        result.reshape(outgoing.shape), EP, 0, 0, tiled=True
    ).reshape(-1, model_slice)
    mine = kernel_call(
        combine_body,
        [struct((8, rows_dev, model_slice), bf16)],
        (ids, back, combine_table),
        scalars=1,
    )[0]
    moe_out = lax.all_to_all(mine, SEG, 0, 0, tiled=True).transpose(1, 0, 2).reshape(rows_dev, -1)

    attn_out = kernel_call(
        norm_body,
        [struct((tokens, all_features), bf16)],
        (ids, *mixed, out_gain.reshape(1, -1)),
        scalars=1,
    )[0]
    return attn_out, moe_out


def solution(mesh):
    torus = Mesh(mesh.devices.reshape(4, 2, 8, 4), SEG_EP)
    placed = (
        P(SEG_EP, None),
        P(SEG_EP, None),
        P(SEG_EP, None),
        P(SEG, EP),
        P(),
        P(EP, SEG),
        P(SEG_EP, None),
        P(SEG_EP, None),
        P(EP, None, SEG),
        P(EP, SEG, None),
    )
    return jax.shard_map(
        on_device,
        mesh=torus,
        in_specs=placed,
        out_specs=(P(SEG_EP, None), P(SEG_EP, None)),
        check_vma=False,
    )
```

time: 524 us -> 305 us (0.58)
  local copies, waits for them, and re-layouts: 115 us -> 23.8 us
  waiting for transfers between devices: 194 us -> 132 us
  matrix products: 54.1 us -> 0.14 us
  blocking collectives: 43.2 us -> 0 us
  starting transfers between devices: 54.8 us -> 90.3 us
  Pallas kernels: 0 us -> 34.2 us
  other arithmetic: 36.2 us -> 2.25 us
  between operations: 14 us -> 21.6 us
  loops' own time: 6.62 us -> 0 us
    ppermute x0 -> x34, waiting for transfers between devices: none -> 96.7 us  [shifted(): return lax.ppermute(v, axis, [(i, (i + by) % n) for i in range(n)])]
    reduce_scatter x3 -> x0, waiting for transfers between devices: 62.1 us -> none  [the longest x2 61.5 us: scatter_axes(): x = lax.psum_scatter(x, axis, scatter_dimension=dim, tiled=True)]
    all_to_all x6, waiting for transfers between devices: 86.6 us -> 28.3 us  [the longest x1 17.6 us: on_device(): lax.all_to_all(result.reshape(outgoing.shape), EP, 0, 0, tiled=True)]
    dot_general x11 -> x1, matrix products: 54.1 us -> 0.14 us  [on_device(): jnp.dot(decay, upto, precision=lax.Precision.HIGHEST)]
    dynamic_update_slice x8 -> x0, local copies, waits for them, and re-layouts: 52.2 us -> none  [on_device(): lax.map(block_mix, starts).reshape(seg_length, heads_local, head_dim)]
    ppermute x0 -> x34, starting transfers between devices: none -> 49.2 us  [shifted(): return lax.ppermute(v, axis, [(i, (i + by) % n) for i in range(n)])]
    all_gather x2 -> x1, waiting for transfers between devices: 44.6 us -> 5.84 us  [on_device(): weight_out = lax.all_gather(out_proj, 'z', axis=0, tiled=True)]
    pallas_call x0 -> x13, Pallas kernels: none -> 34.2 us  [kernel_call(): pl.pallas_call(body, out_shape=tuple(outs), grid=() if steps is None else...]
  transfers between devices with their start and end apart: 11 -> 41, of which waited for: 9 -> 26; matrix products, arithmetic and copies ran while one was open for 32% -> 4% of each run, Pallas kernels for 0% -> 5%
where the time goes in v1:
time: 305 us; the launch traced here: 304 us
  waiting for transfers between devices  132 us (43%)
  starting transfers between devices  90.3 us (30%)
  Pallas kernels  34.2 us (11%)
  local copies, waits for them, and re-layouts  23.8 us (8%)
  between operations  21.6 us (7%)
    ppermute x34, waiting for transfers between devices, shifted(): return lax.ppermute(v, axis, [(i, (i + by) % n) for i in range(n)])  96.7 us
    ppermute x34, starting transfers between devices, shifted(): return lax.ppermute(v, axis, [(i, (i + by) % n) for i in range(n)])  49.2 us
    pallas_call x13, Pallas kernels, kernel_call(): pl.pallas_call(body, out_shape=tuple(outs), grid=() if steps is None else...  34.2 us
    all_to_all x1, waiting for transfers between devices, on_device(): lax.all_to_all(result.reshape(outgoing.shape), EP, 0, 0, tiled=True)  17.6 us
    unnamed x64, local copies, waits for them, and re-layouts  12.5 us
    all_to_all x1, starting transfers between devices, on_device(): lax.all_to_all(result.reshape(outgoing.shape), EP, 0, 0, tiled=True)  9.21 us
    all_to_all x1, starting transfers between devices, on_device(): lax.all_to_all(rel_own.transpose(1, 0, 2), 'z', 0, 0, tiled=True)  8.19 us
    all_to_all x1, waiting for transfers between devices, on_device(): states = lax.all_to_all(states, 'z', 0, 0, tiled=True)  7.71 us
  transfers between devices with their start and end apart: 41, of which 26 were waited for; matrix products, arithmetic and copies ran while one was open for 4% of the time, Pallas kernels for 5%

profile of v1, /device:TPU:1, one launch (start us, length us, event | category | flops | bytes accessed | tf_op | source)
XLA Modules:
  0.0 303.8 jit_solution(2304237421855855246)
XLA Ops:
  22.4 8.2 %all-to-all-start = ((f32[8,2,256]{2,1,0:T(2,128)}), f32[8,2,256]{2,1,0:T(2,128)S(1)}, u32[]{:S(2)}, u32[]{:S(2)}) async-start(f32[8,2,256]{2,1,0:T(2,128)} %copy.81), calls=%async_computation | async-start | bytes 32768 | tf_op jit(solution)/shard_map/all_to_all | solution.py:345
  48.4 4.5 %shard_map.116 = bf16[8,256,128]{2,1,0:T(8,128)(2,1)} custom-call(bf16[2,64,2048]{2,1,0:T(8,128)(2,1)} %copy-done.2, bf16[2,64,2048]{2,1,0:T(8,128)(2,1)} %collective-permute-done.kv1, bf16[2,64,2048]{2,1,0:T(8,128)(2,1)} %collective-permute-done.4.kv2, bf16[2,64,2048]{2,1,0:T(8,128)(2,1)} %collective-permute-done.5.kv3, f32[4,256,4]{2,1,0:T(8,128)S(1)} %bitcast.62, ...), custom_call_target="tpu_custom_call" | custom-call | flops 134217728 | bytes 2637888 | tf_op jit(solution)/shard_map/pallas_call | solution.py:45
  52.9 5.8 %all-gather.2.cloned.1.call-done.weight = bf16[2048,768]{1,0:T(8,128)(2,1)} async-done(((bf16[256,768]{1,0:T(8,128)(2,1)}), bf16[2048,768]{1,0:T(8,128)(2,1)}) %all-gather.2.cloned.1.call-update) | async-done | bytes 3145744 | tf_op jit(solution)/shard_map/all_gather | solution.py:323
  58.8 4.2 %all-to-all-start.1 = ((bf16[8,256,128]{2,1,0:T(8,128)(2,1)}), bf16[8,256,128]{2,1,0:T(8,128)(2,1)S(1)}, u32[]{:S(2)}, u32[]{:S(2)}) async-start(bf16[8,256,128]{2,1,0:T(8,128)(2,1)} %shard_map.116), calls=%async_computation.1 | async-start | bytes 1048576 | tf_op jit(solution)/shard_map/all_to_all | solution.py:374
  66.4 5.2 %collective-permute-done.7.w2 = bf16[288,1536]{1,0:T(8,128)(2,1)} collective-permute-done((bf16[288,1536]{1,0:T(8,128)(2,1)}, bf16[288,1536]{1,0:T(8,128)(2,1)}, u32[]{:S(2)}, u32[]{:S(2)}) %collective-permute-start.7) | collective-permute-done | bytes 884768 | tf_op jit(solution)/shard_map/ppermute | solution.py:22
  73.2 7.7 %all-to-all-done.1.s = bf16[8,256,128]{2,1,0:T(8,128)(2,1)S(1)} async-done(((bf16[8,256,128]{2,1,0:T(8,128)(2,1)}), bf16[8,256,128]{2,1,0:T(8,128)(2,1)S(1)}, u32[]{:S(2)}, u32[]{:S(2)}) %all-to-all-start.1) | async-done | bytes 524320 | tf_op jit(solution)/shard_map/all_to_all | solution.py:374
  85.1 8.2 %collective-permute-done.11 = bf16[272,128]{1,0:T(8,128)(2,1)S(1)} collective-permute-done((bf16[272,128]{1,0:T(8,128)(2,1)S(1)}, bf16[272,128]{1,0:T(8,128)(2,1)S(1)}, u32[]{:S(2)}, u32[]{:S(2)}) %collective-permute-start.11) | collective-permute-done | bytes 69664 | tf_op jit(solution)/shard_map/ppermute | solution.py:22
  93.6 6.2 %collective-permute-start.12 = (bf16[1088,128]{1,0:T(8,128)(2,1)S(1)}, bf16[1088,128]{1,0:T(8,128)(2,1)S(1)}, u32[]{:S(2)}, u32[]{:S(2)}) collective-permute-start(bf16[1088,128]{1,0:T(8,128)(2,1)S(1)} %pad_maximum_fusion.g0), channel_id=1, source_target_pairs={{0,32},{32,0},{1,33},{33,1},{2,34},{34,2},{3,35},{35,3},{4,36},{36... | collective-permute-start | bytes 835592 | tf_op jit(solution)/shard_map/ppermute | solution.py:22
  103.9 6.4 %all-to-all-start.2 = ((bf16[8,256,128]{2,1,0:T(8,128)(2,1)}), bf16[8,256,128]{2,1,0:T(8,128)(2,1)}, u32[]{:S(2)}, u32[]{:S(2)}) async-start(bf16[8,256,128]{2,1,0:T(8,128)(2,1)} %shard_map.118), calls=%async_computation.2 | async-start | bytes 1048576 | tf_op jit(solution)/shard_map/all_to_all | solution.py:395
  117.4 4.7 %collective-permute-done.1.q1 = bf16[64,2048]{1,0:T(8,128)(2,1)S(1)} collective-permute-done((bf16[64,2048]{1,0:T(8,128)(2,1)}, bf16[64,2048]{1,0:T(8,128)(2,1)S(1)}, u32[]{:S(2)}, u32[]{:S(2)}) %collective-permute-start.1) | collective-permute-done | bytes 262176 | tf_op jit(solution)/shard_map/ppermute | solution.py:22
  122.1 5.1 %collective-permute-done.2.q2 = bf16[64,2048]{1,0:T(8,128)(2,1)S(1)} collective-permute-done((bf16[64,2048]{1,0:T(8,128)(2,1)}, bf16[64,2048]{1,0:T(8,128)(2,1)S(1)}, u32[]{:S(2)}, u32[]{:S(2)}) %collective-permute-start.2) | collective-permute-done | bytes 262176 | tf_op jit(solution)/shard_map/ppermute | solution.py:22
  128.6 4.6 %shard_map.115.inside = f32[256,2048]{1,0:T(8,128)S(1)} custom-call(s32[3]{0:T(128)S(1)} %copy-done.13, bf16[64,2048]{1,0:T(8,128)(2,1)} %copy-done.3, bf16[64,2048]{1,0:T(8,128)(2,1)} %copy-done.23, bf16[64,2048]{1,0:T(8,128)(2,1)} %copy-done.24, bf16[64,2048]{1,0:T(8,128)(2,1)} %copy-done.25, bf16[2,64,2048]{2,1,0:T(8,128)(2,1)} %copy-done.2, ...), custom_call_target="tpu_custom_call" | custom-call | flops 536870912 | bytes 5275660 | tf_op jit(solution)/shard_map/pallas_call | solution.py:45
  134.5 5.7 %shard_map.119 = (bf16[64,2048]{1,0:T(8,128)(2,1)S(1)}, bf16[64,2048]{1,0:T(8,128)(2,1)S(1)}, bf16[64,2048]{1,0:T(8,128)(2,1)S(1)}, bf16[64,2048]{1,0:T(8,128)(2...) custom-call(f32[256,2048]{1,0:T(8,128)} %copy-done, bf16[64,2048]{1,0:T(8,128)(2,1)} %copy-done.3, ...), custom_call_target="tpu_custom_call" | custom-call | flops 134217728 | bytes 4898816 | tf_op jit(solution)/shard_map/pallas_call | solution.py:45
  141.9 6.9 %collective-permute-done.17 = bf16[32,2176]{1,0:T(8,128)(2,1)S(1)} collective-permute-done((bf16[32,2176]{1,0:T(8,128)(2,1)S(1)}, bf16[32,2176]{1,0:T(8,128)(2,1)S(1)}, u32[]{:S(2)}, u32[]{:S(2)}) %collective-permute-start.17) | collective-permute-done | bytes 139296 | tf_op jit(solution)/shard_map/ppermute | solution.py:22
  171.6 7.0 %all-to-all-start.3 = ((bf16[32,16,768]{2,1,0:T(8,128)(2,1)}), bf16[32,16,768]{2,1,0:T(8,128)(2,1)S(1)}, u32[]{:S(2)}, u32[]{:S(2)}) async-start(bf16[32,16,768]{2,1,0:T(8,128)(2,1)} %shard_map.122), calls=%async_computation.3 | async-start | bytes 1572864 | tf_op jit(solution)/shard_map/all_to_all | solution.py:431
  181.8 18.8 %collective-permute-done.24.w1 = bf16[288,1536]{1,0:T(8,128)(2,1)} collective-permute-done((bf16[288,1536]{1,0:T(8,128)(2,1)}, bf16[288,1536]{1,0:T(8,128)(2,1)}, u32[]{:S(2)}, u32[]{:S(2)}) %collective-permute-start.24) | collective-permute-done | bytes 884768 | tf_op jit(solution)/shard_map/ppermute | solution.py:22
  211.7 6.0 %collective-permute-done.27 = bf16[288,512]{1,0:T(8,128)(2,1)S(1)} collective-permute-done((bf16[288,512]{1,0:T(8,128)(2,1)S(1)}, bf16[288,512]{1,0:T(8,128)(2,1)S(1)}, u32[]{:S(2)}, u32[]{:S(2)}) %collective-permute-start.27) | collective-permute-done | bytes 294944 | tf_op jit(solution)/shard_map/ppermute | solution.py:22
  220.5 6.7 %collective-permute-done.29 = bf16[288,512]{1,0:T(8,128)(2,1)S(1)} collective-permute-done((bf16[288,512]{1,0:T(8,128)(2,1)S(1)}, bf16[288,512]{1,0:T(8,128)(2,1)S(1)}, u32[]{:S(2)}, u32[]{:S(2)}) %collective-permute-start.29) | collective-permute-done | bytes 294944 | tf_op jit(solution)/shard_map/ppermute | solution.py:22
  228.9 6.3 %collective-permute-done.32.h3 = bf16[288,512]{1,0:T(8,128)(2,1)S(1)} collective-permute-done((bf16[288,512]{1,0:T(8,128)(2,1)S(1)}, bf16[288,512]{1,0:T(8,128)(2,1)S(1)}, u32[]{:S(2)}, u32[]{:S(2)}) %collective-permute-start.32) | collective-permute-done | bytes 294944 | tf_op jit(solution)/shard_map/ppermute | solution.py:22
  236.0 8.3 %collective-permute-done.30.h1 = bf16[288,512]{1,0:T(8,128)(2,1)S(1)} collective-permute-done((bf16[288,512]{1,0:T(8,128)(2,1)S(1)}, bf16[288,512]{1,0:T(8,128)(2,1)S(1)}, u32[]{:S(2)}, u32[]{:S(2)}) %collective-permute-start.30) | collective-permute-done | bytes 294944 | tf_op jit(solution)/shard_map/ppermute | solution.py:22
  244.3 5.2 %shard_map.124 = (f32[512,768]{1,0:T(8,128)S(1)}, bf16[512,768]{1,0:T(8,128)(2,1)S(1)}) custom-call(s32[3]{0:T(128)S(1)} %copy-done.14, bf16[288,512]{1,0:T(8,128)(2,1)S(1)} %multiply_convert_fusion.h0, bf16[288,512]{1,0:T(8,128)(2,1)S(1)} %collective-permute-done.30.h1, bf16[288,512]{1,0:T(8,128)(2,1)S(1)} %collective-permute-done.31.h2, ...), custom_call_target="tpu_custom_call" | custom-call | flops 1811939328 | bytes 7077900 | tf_op jit(solution)/shard_map/pallas_call | solution.py:45
  253.1 9.2 %all-to-all-start.4 = ((bf16[32,16,768]{2,1,0:T(8,128)(2,1)}), bf16[32,16,768]{2,1,0:T(8,128)(2,1)S(1)}, u32[]{:S(2)}, u32[]{:S(2)}) async-start(bf16[32,16,768]{2,1,0:T(8,128)(2,1)} %bitcast.36), calls=%async_computation.4 | async-start | bytes 1572864 | tf_op jit(solution)/shard_map/all_to_all | solution.py:456
  266.0 17.6 %all-to-all-done.4 = bf16[32,16,768]{2,1,0:T(8,128)(2,1)S(1)} async-done(((bf16[32,16,768]{2,1,0:T(8,128)(2,1)}), bf16[32,16,768]{2,1,0:T(8,128)(2,1)S(1)}, u32[]{:S(2)}, u32[]{:S(2)}) %all-to-all-start.4) | async-done | bytes 786464 | tf_op jit(solution)/shard_map/all_to_all | solution.py:456
  285.2 6.1 %all-to-all-start.5 = ((bf16[8,8,768]{2,1,0:T(8,128)(2,1)}), bf16[8,8,768]{2,1,0:T(8,128)(2,1)S(1)}, u32[]{:S(2)}, u32[]{:S(2)}) async-start(bf16[8,8,768]{2,1,0:T(8,128)(2,1)} %shard_map.125), calls=%async_computation.5 | async-start | bytes 196608 | tf_op jit(solution)/shard_map/all_to_all | solution.py:465
  (187 shorter events, 107.7 us)
Async XLA Ops:
  7.2 51.6 %all-gather.2.cloned.1.call-start = ((), (), s32[]{:S(2)}) async-start(), calls=%async_computation.6 | async-start | bytes 3538944 | tf_op jit(solution)/shard_map/all_gather | solution.py:323
  12.1 35.2 %collective-permute-start = (bf16[2,64,2048]{2,1,0:T(8,128)(2,1)S(1)}, bf16[2,64,2048]{2,1,0:T(8,128)(2,1)}, u32[]{:S(2)}, u32[]{:S(2)}) collective-permute-start(bf16[2,64,2048]{2,1,0:T(8,128)(2,1)S(1)} %get-tuple-element.51), channel_id=1, source_target_pairs={{0,1},{1,2},{2,3},{3,0},{4,5},{5,6},{6,7},{7,4},{8,9},{9,10},{10,1... | collective-permute-start | bytes 1572872 | tf_op jit(solution)/shard_map/ppermute | solution.py:22
  14.1 34.3 %collective-permute-start.4 = (bf16[2,64,2048]{2,1,0:T(8,128)(2,1)S(1)}, bf16[2,64,2048]{2,1,0:T(8,128)(2,1)}, u32[]{:S(2)}, u32[]{:S(2)}) collective-permute-start(bf16[2,64,2048]{2,1,0:T(8,128)(2,1)S(1)} %get-tuple-element.60), channel_id=1, source_target_pairs={{0,2},{1,3},{2,0},{3,1},{4,6},{5,7},{6,4},{7,5},{8,10},{9,11},{10,... | collective-permute-start | bytes 1572872 | tf_op jit(solution)/shard_map/ppermute | solution.py:22
  16.6 31.9 %collective-permute-start.5 = (bf16[2,64,2048]{2,1,0:T(8,128)(2,1)S(1)}, bf16[2,64,2048]{2,1,0:T(8,128)(2,1)}, u32[]{:S(2)}, u32[]{:S(2)}) collective-permute-start(bf16[2,64,2048]{2,1,0:T(8,128)(2,1)S(1)} %get-tuple-element.61), channel_id=1, source_target_pairs={{0,3},{1,0},{2,1},{3,2},{4,7},{5,4},{6,5},{7,6},{8,11},{9,8},{10,9... | collective-permute-start | bytes 1572872 | tf_op jit(solution)/shard_map/ppermute | solution.py:22
  22.4 24.1 %all-to-all-start = ((f32[8,2,256]{2,1,0:T(2,128)}), f32[8,2,256]{2,1,0:T(2,128)S(1)}, u32[]{:S(2)}, u32[]{:S(2)}) async-start(f32[8,2,256]{2,1,0:T(2,128)} %copy.81), calls=%async_computation | async-start | bytes 32768 | tf_op jit(solution)/shard_map/all_to_all | solution.py:345
  30.6 35.8 %collective-permute-start.6 = (bf16[288,1536]{1,0:T(8,128)(2,1)}, bf16[288,1536]{1,0:T(8,128)(2,1)}, u32[]{:S(2)}, u32[]{:S(2)}) collective-permute-start(bf16[288,1536]{1,0:T(8,128)(2,1)} %get-tuple-element.65), channel_id=1, source_target_pairs={{0,64},{64,128},{128,192},{192,0},{1,65},{65,129},{129,193},{193,1... | collective-permute-start | bytes 2654216 | tf_op jit(solution)/shard_map/ppermute | solution.py:22
  31.9 39.8 %collective-permute-start.7 = (bf16[288,1536]{1,0:T(8,128)(2,1)}, bf16[288,1536]{1,0:T(8,128)(2,1)}, u32[]{:S(2)}, u32[]{:S(2)}) collective-permute-start(bf16[288,1536]{1,0:T(8,128)(2,1)} %get-tuple-element.66), channel_id=1, source_target_pairs={{0,128},{64,192},{128,0},{192,64},{1,129},{65,193},{129,1},{193,65... | collective-permute-start | bytes 2654216 | tf_op jit(solution)/shard_map/ppermute | solution.py:22
  47.3 25.9 %collective-permute-start.8 = (bf16[288,1536]{1,0:T(8,128)(2,1)}, bf16[288,1536]{1,0:T(8,128)(2,1)}, u32[]{:S(2)}, u32[]{:S(2)}) collective-permute-start(bf16[288,1536]{1,0:T(8,128)(2,1)} %get-tuple-element.67), channel_id=1, source_target_pairs={{0,192},{64,0},{128,64},{192,128},{1,193},{65,1},{129,65},{193,129... | collective-permute-start | bytes 2654216 | tf_op jit(solution)/shard_map/ppermute | solution.py:22
  58.8 22.1 %all-to-all-start.1 = ((bf16[8,256,128]{2,1,0:T(8,128)(2,1)}), bf16[8,256,128]{2,1,0:T(8,128)(2,1)S(1)}, u32[]{:S(2)}, u32[]{:S(2)}) async-start(bf16[8,256,128]{2,1,0:T(8,128)(2,1)} %shard_map.116), calls=%async_computation.1 | async-start | bytes 1048576 | tf_op jit(solution)/shard_map/all_to_all | solution.py:374
  63.1 36.7 %collective-permute-start.13 = (bf16[288,1536]{1,0:T(8,128)(2,1)}, bf16[288,1536]{1,0:T(8,128)(2,1)}, u32[]{:S(2)}, u32[]{:S(2)}) collective-permute-start(bf16[288,1536]{1,0:T(8,128)(2,1)} %get-tuple-element.69), channel_id=1, source_target_pairs={{0,128},{64,192},{128,0},{192,64},{1,129},{65,193},{129,1},{193,65... | collective-permute-start | bytes 2654216 | tf_op jit(solution)/shard_map/ppermute | solution.py:22
  81.6 11.8 %collective-permute-start.11 = (bf16[272,128]{1,0:T(8,128)(2,1)S(1)}, bf16[272,128]{1,0:T(8,128)(2,1)S(1)}, u32[]{:S(2)}, u32[]{:S(2)}) collective-permute-start(bf16[272,128]{1,0:T(8,128)(2,1)S(1)} %shard_map.117), channel_id=1, source_target_pairs={{0,192},{64,0},{128,64},{192,128},{1,193},{65,1},{129,65},{193,129... | collective-permute-start | bytes 208904 | tf_op jit(solution)/shard_map/ppermute | solution.py:22
  103.9 30.6 %all-to-all-start.2 = ((bf16[8,256,128]{2,1,0:T(8,128)(2,1)}), bf16[8,256,128]{2,1,0:T(8,128)(2,1)}, u32[]{:S(2)}, u32[]{:S(2)}) async-start(bf16[8,256,128]{2,1,0:T(8,128)(2,1)} %shard_map.118), calls=%async_computation.2 | async-start | bytes 1048576 | tf_op jit(solution)/shard_map/all_to_all | solution.py:395
  113.4 13.8 %collective-permute-start.2 = (bf16[64,2048]{1,0:T(8,128)(2,1)}, bf16[64,2048]{1,0:T(8,128)(2,1)S(1)}, u32[]{:S(2)}, u32[]{:S(2)}) collective-permute-start(bf16[64,2048]{1,0:T(8,128)(2,1)} %get-tuple-element.55), channel_id=1, source_target_pairs={{0,2},{1,3},{2,0},{3,1},{4,6},{5,7},{6,4},{7,5},{8,10},{9,11},{10,... | collective-permute-start | bytes 786440 | tf_op jit(solution)/shard_map/ppermute | solution.py:22
  115.4 12.4 %collective-permute-start.3 = (bf16[64,2048]{1,0:T(8,128)(2,1)S(1)}, bf16[64,2048]{1,0:T(8,128)(2,1)S(1)}, u32[]{:S(2)}, u32[]{:S(2)}) collective-permute-start(bf16[64,2048]{1,0:T(8,128)(2,1)S(1)} %get-tuple-element.56), channel_id=1, source_target_pairs={{0,3},{1,0},{2,1},{3,2},{4,7},{5,4},{6,5},{7,6},{8,11},{9,8},{10,9... | collective-permute-start | bytes 786440 | tf_op jit(solution)/shard_map/ppermute | solution.py:22
  171.6 28.9 %all-to-all-start.3 = ((bf16[32,16,768]{2,1,0:T(8,128)(2,1)}), bf16[32,16,768]{2,1,0:T(8,128)(2,1)S(1)}, u32[]{:S(2)}, u32[]{:S(2)}) async-start(bf16[32,16,768]{2,1,0:T(8,128)(2,1)} %shard_map.122), calls=%async_computation.3 | async-start | bytes 1572864 | tf_op jit(solution)/shard_map/all_to_all | solution.py:431
  178.7 21.9 %collective-permute-start.24 = (bf16[288,1536]{1,0:T(8,128)(2,1)}, bf16[288,1536]{1,0:T(8,128)(2,1)}, u32[]{:S(2)}, u32[]{:S(2)}) collective-permute-start(bf16[288,1536]{1,0:T(8,128)(2,1)} %get-tuple-element.82), channel_id=1, source_target_pairs={{0,64},{64,128},{128,192},{192,0},{1,65},{65,129},{129,193},{193,1... | collective-permute-start | bytes 2654216 | tf_op jit(solution)/shard_map/ppermute | solution.py:22
  178.8 21.8 %collective-permute-start.25 = (bf16[288,1536]{1,0:T(8,128)(2,1)}, bf16[288,1536]{1,0:T(8,128)(2,1)}, u32[]{:S(2)}, u32[]{:S(2)}) collective-permute-start(bf16[288,1536]{1,0:T(8,128)(2,1)} %get-tuple-element.83), channel_id=1, source_target_pairs={{0,192},{64,0},{128,64},{192,128},{1,193},{65,1},{129,65},{193,129... | collective-permute-start | bytes 2654216 | tf_op jit(solution)/shard_map/ppermute | solution.py:22
  211.0 16.2 %collective-permute-start.29 = (bf16[288,512]{1,0:T(8,128)(2,1)S(1)}, bf16[288,512]{1,0:T(8,128)(2,1)S(1)}, u32[]{:S(2)}, u32[]{:S(2)}) collective-permute-start(bf16[288,512]{1,0:T(8,128)(2,1)S(1)} %get-tuple-element.92), channel_id=1, source_target_pairs={{0,64},{64,128},{128,192},{192,0},{1,65},{65,129},{129,193},{193,1... | collective-permute-start | bytes 884744 | tf_op jit(solution)/shard_map/ppermute | solution.py:22
  228.2 16.2 %collective-permute-start.30 = (bf16[288,512]{1,0:T(8,128)(2,1)S(1)}, bf16[288,512]{1,0:T(8,128)(2,1)S(1)}, u32[]{:S(2)}, u32[]{:S(2)}) collective-permute-start(bf16[288,512]{1,0:T(8,128)(2,1)S(1)} %multiply_convert_fusion.h0), channel_id=1, source_target_pairs={{0,64},{64,128},{128,192},{192,0},{1,65},{65,129},{129,193},{193,1... | collective-permute-start | bytes 884744 | tf_op jit(solution)/shard_map/ppermute | solution.py:22
  253.1 30.5 %all-to-all-start.4 = ((bf16[32,16,768]{2,1,0:T(8,128)(2,1)}), bf16[32,16,768]{2,1,0:T(8,128)(2,1)S(1)}, u32[]{:S(2)}, u32[]{:S(2)}) async-start(bf16[32,16,768]{2,1,0:T(8,128)(2,1)} %bitcast.36), calls=%async_computation.4 | async-start | bytes 1572864 | tf_op jit(solution)/shard_map/all_to_all | solution.py:456
  262.4 29.0 %collective-permute-start.14 = (bf16[64,2048]{1,0:T(8,128)(2,1)S(1)}, bf16[64,2048]{1,0:T(8,128)(2,1)S(1)}, u32[]{:S(2)}, u32[]{:S(2)}) collective-permute-start(bf16[64,2048]{1,0:T(8,128)(2,1)S(1)} %copy-done.22), channel_id=1, source_target_pairs={{0,3},{1,0},{2,1},{3,2},{4,7},{5,4},{6,5},{7,6},{8,11},{9,8},{10,9... | collective-permute-start | bytes 786440 | tf_op jit(solution)/shard_map/ppermute | solution.py:22
  264.9 26.4 %collective-permute-start.15 = (bf16[64,2048]{1,0:T(8,128)(2,1)S(1)}, bf16[64,2048]{1,0:T(8,128)(2,1)S(1)}, u32[]{:S(2)}, u32[]{:S(2)}) collective-permute-start(bf16[64,2048]{1,0:T(8,128)(2,1)S(1)} %copy-done.20), channel_id=1, source_target_pairs={{0,2},{1,3},{2,0},{3,1},{4,6},{5,7},{6,4},{7,5},{8,10},{9,11},{10,... | collective-permute-start | bytes 786440 | tf_op jit(solution)/shard_map/ppermute | solution.py:22
  265.5 25.9 %collective-permute-start.16 = (bf16[64,2048]{1,0:T(8,128)(2,1)S(1)}, bf16[64,2048]{1,0:T(8,128)(2,1)S(1)}, u32[]{:S(2)}, u32[]{:S(2)}) collective-permute-start(bf16[64,2048]{1,0:T(8,128)(2,1)S(1)} %copy-done.18), channel_id=1, source_target_pairs={{0,1},{1,2},{2,3},{3,0},{4,5},{5,6},{6,7},{7,4},{8,9},{9,10},{10,1... | collective-permute-start | bytes 786440 | tf_op jit(solution)/shard_map/ppermute | solution.py:22
  285.2 11.1 %all-to-all-start.5 = ((bf16[8,8,768]{2,1,0:T(8,128)(2,1)}), bf16[8,8,768]{2,1,0:T(8,128)(2,1)S(1)}, u32[]{:S(2)}, u32[]{:S(2)}) async-start(bf16[8,8,768]{2,1,0:T(8,128)(2,1)} %shard_map.125), calls=%async_computation.5 | async-start | bytes 196608 | tf_op jit(solution)/shard_map/all_to_all | solution.py:465
  (46 other events, 501.6 us)
Sparse Core Ops, SparseCore 0:
  9.8 48.9 all-gather.1

commit v2 on v1

--- a/solution.py
+++ b/solution.py
@@ -38,7 +38,7 @@
     if steps is not None:
         args = [
             pltpu.with_memory_space_constraint(a, pltpu.HBM)
-            if i >= scalars and a.size * a.dtype.itemsize >= 1 << 18
+            if i >= scalars and a.dtype == bf16 and a.size >= 1 << 17
             else a
             for i, a in enumerate(args)
         ]
@@ -311,14 +311,16 @@
     rows_dev = experts.shape[0]
     expert_count = 4 * n_z // 2
 
+    def over_x(pieces):
+        return [pieces[0]] + [shifted(pieces[d], "x", d) for d in range(1, 4)]
+
     kv_out = kernel_call(
         pack_pair_body, [struct((2, tokens, features), bf16)] * 4, (ids, keys, values), scalars=1
     )
     kv_out = list(kv_out)
-    kv = [None] + [shifted(kv_out[d], "x", d) for d in range(1, 4)]
+    kv = over_x(kv_out)
     queries, kv[1] = lax.optimization_barrier((queries, kv[1]))
     q_out = kernel_call(pack_body, [struct((tokens, features), bf16)] * 4, (ids, queries), scalars=1)
-    q = [q_out[0]] + [shifted(q_out[d], "x", d) for d in range(1, 4)]
 
     weight_out = lax.all_gather(out_proj, "z", axis=0, tiled=True)
 
@@ -367,11 +369,18 @@
         steps=steps,
         blocks=(2, 2, 2, 2, 0, 0, 0),
     )[0]
-    states, weight_out, *down = lax.optimization_barrier(
-        (states, weight_out, *sliced(down_weight[0]))
-    )
-    down = over_y(down)
+    states, weight_out, *rest = lax.optimization_barrier(
+        (states, weight_out, *q_out, *sliced(down_weight[0]))
+    )
+    q = over_x(rest[:4])
+    down = over_y(rest[4:])
     states = lax.all_to_all(states, "z", 0, 0, tiled=True)
+    states, *rest = lax.optimization_barrier((states, *up, *q))
+    up, q = rest[:4], rest[4:]
+    local = kernel_call(
+        group_state_body, [struct((PAIR + 16, HEAD), bf16)], (chunk_decay, states, info), scalars=1
+    )[0]
+    groups = over_seg(local)
     inside = kernel_call(
         inside_body,
         [struct((length, features), f32)],
@@ -381,11 +390,6 @@
         steps=steps,
         blocks=(1,) * 4 + (2,) * 4 + (0, 0, 1),
     )[0]
-    states, *up = lax.optimization_barrier((states, *up))
-    local = kernel_call(
-        group_state_body, [struct((PAIR + 16, HEAD), bf16)], (chunk_decay, states, info), scalars=1
-    )[0]
-    *groups, down[2] = lax.optimization_barrier((*over_seg(local), down[2]))
     prefix = kernel_call(
         prefix_body,
         [struct((n_z, PAIR, HEAD), bf16)],
@@ -416,6 +420,8 @@
         blocks=(1,) * 5 + (0, 0, 1) + (1,) * 4 + (None, None),
     )
 
+    rows, down[2] = lax.optimization_barrier((rows, down[2]))
+
     terms = kernel_call(
         project_body,
         [struct((8 * rows_dev, model_slice + HEAD), bf16)] * 4,

time: 305 us -> 283 us (0.928)
  waiting for transfers between devices: 132 us -> 121 us
  starting transfers between devices: 90.3 us -> 82.2 us
  local copies, waits for them, and re-layouts: 23.8 us -> 19.9 us
    all_to_all x1, waiting for transfers between devices: 0.01 us -> 12.7 us  [on_device(): prefix = lax.all_to_all(prefix, 'z', 0, 0, tiled=True)]
    ppermute x34, waiting for transfers between devices: 96.7 us -> 86.4 us  [shifted(): return lax.ppermute(v, axis, [(i, (i + by) % n) for i in range(n)])]
    all_to_all x1, waiting for transfers between devices: 7.71 us -> 0.52 us  [on_device(): states = lax.all_to_all(states, 'z', 0, 0, tiled=True)]
    ppermute x34, starting transfers between devices: 49.2 us -> 42.5 us  [shifted(): return lax.ppermute(v, axis, [(i, (i + by) % n) for i in range(n)])]
    all_gather x1, waiting for transfers between devices: 5.84 us -> 0.56 us  [on_device(): weight_out = lax.all_gather(out_proj, 'z', axis=0, tiled=True)]
    unnamed x64 -> x60, local copies, waits for them, and re-layouts: 12.5 us -> 8.88 us
  transfers between devices with their start and end apart: 41 -> 41, of which waited for: 26 -> 27; matrix products, arithmetic and copies ran while one was open for 4% -> 4% of each run, Pallas kernels for 5% -> 7%
where the time goes in v2:
time: 283 us; the launch traced here: 282 us
  waiting for transfers between devices  121 us (43%)
  starting transfers between devices  82.2 us (29%)
  Pallas kernels  34 us (12%)
  between operations  21.7 us (8%)
  local copies, waits for them, and re-layouts  19.9 us (7%)
    ppermute x34, waiting for transfers between devices, shifted(): return lax.ppermute(v, axis, [(i, (i + by) % n) for i in range(n)])  86.4 us
    ppermute x34, starting transfers between devices, shifted(): return lax.ppermute(v, axis, [(i, (i + by) % n) for i in range(n)])  42.5 us
    pallas_call x13, Pallas kernels, kernel_call(): pl.pallas_call(body, out_shape=tuple(outs), grid=() if steps is None else...  34 us
    all_to_all x1, waiting for transfers between devices, on_device(): lax.all_to_all(result.reshape(outgoing.shape), EP, 0, 0, tiled=True)  17.6 us
    all_to_all x1, waiting for transfers between devices, on_device(): prefix = lax.all_to_all(prefix, 'z', 0, 0, tiled=True)  12.7 us
    all_to_all x1, starting transfers between devices, on_device(): lax.all_to_all(result.reshape(outgoing.shape), EP, 0, 0, tiled=True)  9.22 us
    unnamed x60, local copies, waits for them, and re-layouts  8.88 us
    all_to_all x1, starting transfers between devices, on_device(): lax.all_to_all(rel_own.transpose(1, 0, 2), 'z', 0, 0, tiled=True)  8.19 us
  transfers between devices with their start and end apart: 41, of which 27 were waited for; matrix products, arithmetic and copies ran while one was open for 4% of the time, Pallas kernels for 7%

profile of v2, /device:TPU:1, one launch (start us, length us, event | category | flops | bytes accessed | tf_op | source)
XLA Modules:
  0.0 281.6 jit_solution(592463102862903368)
XLA Ops:
  18.7 3.9 %dynamic-slice_bitcast_fusion.4 = (bf16[288,1536]{1,0:T(8,128)(2,1)}, bf16[288,1536]{1,0:T(8,128)(2,1)}, bf16[288,1536]{1,0:T(8,128)(2,1)}, bf16[288,1536]{1,0:T(8,128)(2,1)}) fusion(bf16[1,6144,288]{1,2,0:T(8,128)(2,1)} %param.18, s32[]{:T(128)S(6)} %select_n.108, s32[]{:T(128)S(6)} %select_n.104, s32[]{:T(128)S(6)} %select_n.102, s32[]{:T(128)S(6)} %select_n.106), kind=kLoop, calls=%fused_computation.5 | loop fusion | bytes 7077904 | tf_op jit(solution)/shard_map/dynamic_slice | solution.py:330
  23.4 8.2 %all-to-all-start = ((f32[8,2,256]{2,1,0:T(2,128)}), f32[8,2,256]{2,1,0:T(2,128)S(1)}, u32[]{:S(2)}, u32[]{:S(2)}) async-start(f32[8,2,256]{2,1,0:T(2,128)} %copy.81), calls=%async_computation | async-start | bytes 32768 | tf_op jit(solution)/shard_map/all_to_all | solution.py:347
  36.1 4.0 %dynamic-slice_bitcast_fusion = (bf16[288,1536]{1,0:T(8,128)(2,1)}, bf16[288,1536]{1,0:T(8,128)(2,1)}, bf16[288,1536]{1,0:T(8,128)(2,1)}, bf16[288,1536]{1,0:T(8,128)(2,1)}) fusion(bf16[1,288,6144]{2,1,0:T(8,128)(2,1)} %param.19, s32[]{:T(128)S(6)} %select_n.108, s32[]{:T(128)S(6)} %select_n.104, s32[]{:T(128)S(6)} %select_n.102, s32[]{:T(128)S(6)} %select_n.106), kind=kLoop, calls=%fused_computation.1 | loop fusion | bytes 7077904 | tf_op jit(solution)/shard_map/dynamic_slice | solution.py:330
  53.5 4.6 %shard_map.114 = bf16[8,256,128]{2,1,0:T(8,128)(2,1)} custom-call(bf16[2,64,2048]{2,1,0:T(8,128)(2,1)} %copy-done.1, bf16[2,64,2048]{2,1,0:T(8,128)(2,1)} %collective-permute-done.kv1, bf16[2,64,2048]{2,1,0:T(8,128)(2,1)} %collective-permute-done.1.kv2, bf16[2,64,2048]{2,1,0:T(8,128)(2,1)} %collective-permute-done.2.kv3, f32[4,256,4]{2,1,0:T(8,128)S(1)} %bitcast.62, ...), custom_call_target="tpu_custom_call" | custom-call | flops 134217728 | bytes 2637888 | tf_op jit(solution)/shard_map/pallas_call | solution.py:45
  58.6 6.2 %all-to-all-start.1 = ((bf16[8,256,128]{2,1,0:T(8,128)(2,1)}), bf16[8,256,128]{2,1,0:T(8,128)(2,1)S(1)}, u32[]{:S(2)}, u32[]{:S(2)}) async-start(bf16[8,256,128]{2,1,0:T(8,128)(2,1)} %shard_map.114), calls=%async_computation.1 | async-start | bytes 1048576 | tf_op jit(solution)/shard_map/all_to_all | solution.py:377
  68.6 4.1 %collective-permute-done.4.w2 = bf16[288,1536]{1,0:T(8,128)(2,1)} collective-permute-done((bf16[288,1536]{1,0:T(8,128)(2,1)}, bf16[288,1536]{1,0:T(8,128)(2,1)}, u32[]{:S(2)}, u32[]{:S(2)}) %collective-permute-start.4) | collective-permute-done | bytes 884768 | tf_op jit(solution)/shard_map/ppermute | solution.py:22
  73.2 3.1 %collective-permute-done.7.q2 = bf16[64,2048]{1,0:T(8,128)(2,1)} collective-permute-done((bf16[64,2048]{1,0:T(8,128)(2,1)S(1)}, bf16[64,2048]{1,0:T(8,128)(2,1)}, u32[]{:S(2)}, u32[]{:S(2)}) %collective-permute-start.7) | collective-permute-done | bytes 262176 | tf_op jit(solution)/shard_map/ppermute | solution.py:22
  86.7 5.9 %collective-permute-start.12 = (bf16[1088,128]{1,0:T(8,128)(2,1)S(1)}, bf16[1088,128]{1,0:T(8,128)(2,1)S(1)}, u32[]{:S(2)}, u32[]{:S(2)}) collective-permute-start(bf16[1088,128]{1,0:T(8,128)(2,1)S(1)} %pad_maximum_fusion.g0), channel_id=1, source_target_pairs={{0,32},{32,0},{1,33},{33,1},{2,34},{34,2},{3,35},{35,3},{4,36},{36... | collective-permute-start | bytes 835592 | tf_op jit(solution)/shard_map/ppermute | solution.py:22
  95.4 4.7 %all-to-all-start.2 = ((bf16[8,256,128]{2,1,0:T(8,128)(2,1)}), bf16[8,256,128]{2,1,0:T(8,128)(2,1)}, u32[]{:S(2)}, u32[]{:S(2)}) async-start(bf16[8,256,128]{2,1,0:T(8,128)(2,1)} %shard_map.118), calls=%async_computation.2 | async-start | bytes 1048576 | tf_op jit(solution)/shard_map/all_to_all | solution.py:399
  100.9 4.6 %shard_map.116.inside = f32[256,2048]{1,0:T(8,128)S(1)} custom-call(s32[3]{0:T(128)S(1)} %pad_add_fusion.ids, bf16[64,2048]{1,0:T(8,128)(2,1)} %copy-done.2, bf16[64,2048]{1,0:T(8,128)(2,1)} %copy-done.23, bf16[64,2048]{1,0:T(8,128)(2,1)} %collective-permute-done.7.q2, bf16[64,2048]{1,0:T(8,128)(2,1)} %collective-permute-done.8.q3, ...), custom_call_target="tpu_custom_call" | custom-call | flops 536870912 | bytes 5275660 | tf_op jit(solution)/shard_map/pallas_call | solution.py:45
  105.5 12.7 %all-to-all-done.2.prefix = bf16[8,256,128]{2,1,0:T(8,128)(2,1)} async-done(((bf16[8,256,128]{2,1,0:T(8,128)(2,1)}), bf16[8,256,128]{2,1,0:T(8,128)(2,1)}, u32[]{:S(2)}, u32[]{:S(2)}) %all-to-all-start.2) | async-done | bytes 524320 | tf_op jit(solution)/shard_map/all_to_all | solution.py:399
  118.2 5.5 %shard_map.119 = (bf16[64,2048]{1,0:T(8,128)(2,1)S(1)}, bf16[64,2048]{1,0:T(8,128)(2,1)S(1)}, bf16[64,2048]{1,0:T(8,128)(2,1)S(1)}, bf16[64,2048]{1,0:T(8,128)(2...) custom-call(f32[256,2048]{1,0:T(8,128)S(1)} %shard_map.116.inside, bf16[64,2048]{1,0:T(8,128)(2,1)} %copy-done.2, ...), custom_call_target="tpu_custom_call" | custom-call | flops 134217728 | bytes 4898816 | tf_op jit(solution)/shard_map/pallas_call | solution.py:45
  125.5 8.9 %collective-permute-done.17 = bf16[32,2176]{1,0:T(8,128)(2,1)S(1)} collective-permute-done((bf16[32,2176]{1,0:T(8,128)(2,1)S(1)}, bf16[32,2176]{1,0:T(8,128)(2,1)S(1)}, u32[]{:S(2)}, u32[]{:S(2)}) %collective-permute-start.17) | collective-permute-done | bytes 139296 | tf_op jit(solution)/shard_map/ppermute | solution.py:22
  151.7 5.3 %all-to-all-start.3 = ((bf16[32,16,768]{2,1,0:T(8,128)(2,1)}), bf16[32,16,768]{2,1,0:T(8,128)(2,1)S(1)}, u32[]{:S(2)}, u32[]{:S(2)}) async-start(bf16[32,16,768]{2,1,0:T(8,128)(2,1)} %shard_map.122), calls=%async_computation.3 | async-start | bytes 1572864 | tf_op jit(solution)/shard_map/all_to_all | solution.py:437
  160.1 18.2 %collective-permute-done.24.w1 = bf16[288,1536]{1,0:T(8,128)(2,1)} collective-permute-done((bf16[288,1536]{1,0:T(8,128)(2,1)}, bf16[288,1536]{1,0:T(8,128)(2,1)}, u32[]{:S(2)}, u32[]{:S(2)}) %collective-permute-start.24) | collective-permute-done | bytes 884768 | tf_op jit(solution)/shard_map/ppermute | solution.py:22
  182.9 3.5 %shard_map.123 = (bf16[288,512]{1,0:T(8,128)(2,1)S(1)}, bf16[288,512]{1,0:T(8,128)(2,1)S(1)}, bf16[288,512]{1,0:T(8,128)(2,1)S(1)}, bf16[288,512]{1,0:T(8,128)(2,1)S(1)}) custom-call(s32[3]{0:T(128)S(1)} %pad_add_fusion.ids, bf16[512,768]{1,0:T(8,128)(2,1)S(1)} %bitcast.68, bf16[512,768]{1,0:T(8,128)(2,1)S(1)} %collective-permute-done.26.other, ...), custom_call_target="tpu_custom_call" | custom-call | flops 1811939328 | bytes 6291468 | tf_op jit(solution)/shard_map/pallas_call | solution.py:45
  189.5 6.0 %collective-permute-done.27 = bf16[288,512]{1,0:T(8,128)(2,1)S(1)} collective-permute-done((bf16[288,512]{1,0:T(8,128)(2,1)S(1)}, bf16[288,512]{1,0:T(8,128)(2,1)S(1)}, u32[]{:S(2)}, u32[]{:S(2)}) %collective-permute-start.27) | collective-permute-done | bytes 294944 | tf_op jit(solution)/shard_map/ppermute | solution.py:22
  198.3 6.7 %collective-permute-done.29 = bf16[288,512]{1,0:T(8,128)(2,1)S(1)} collective-permute-done((bf16[288,512]{1,0:T(8,128)(2,1)S(1)}, bf16[288,512]{1,0:T(8,128)(2,1)S(1)}, u32[]{:S(2)}, u32[]{:S(2)}) %collective-permute-start.29) | collective-permute-done | bytes 294944 | tf_op jit(solution)/shard_map/ppermute | solution.py:22
  206.8 6.3 %collective-permute-done.32.h3 = bf16[288,512]{1,0:T(8,128)(2,1)S(1)} collective-permute-done((bf16[288,512]{1,0:T(8,128)(2,1)S(1)}, bf16[288,512]{1,0:T(8,128)(2,1)S(1)}, u32[]{:S(2)}, u32[]{:S(2)}) %collective-permute-start.32) | collective-permute-done | bytes 294944 | tf_op jit(solution)/shard_map/ppermute | solution.py:22
  213.9 8.3 %collective-permute-done.30.h1 = bf16[288,512]{1,0:T(8,128)(2,1)S(1)} collective-permute-done((bf16[288,512]{1,0:T(8,128)(2,1)S(1)}, bf16[288,512]{1,0:T(8,128)(2,1)S(1)}, u32[]{:S(2)}, u32[]{:S(2)}) %collective-permute-start.30) | collective-permute-done | bytes 294944 | tf_op jit(solution)/shard_map/ppermute | solution.py:22
  222.2 5.2 %shard_map.124 = (f32[512,768]{1,0:T(8,128)S(1)}, bf16[512,768]{1,0:T(8,128)(2,1)S(1)}) custom-call(s32[3]{0:T(128)S(1)} %pad_add_fusion.ids, bf16[288,512]{1,0:T(8,128)(2,1)S(1)} %multiply_convert_fusion.h0, bf16[288,512]{1,0:T(8,128)(2,1)S(1)} %collective-permute-done.30.h1, bf16[288,512]{1,0:T(8,128)(2,1)S(1)} %collective-permute-done.31.h2, ...), custom_call_target="tpu_custom_call" | custom-call | flops 1811939328 | bytes 7077900 | tf_op jit(solution)/shard_map/pallas_call | solution.py:45
  231.0 9.2 %all-to-all-start.4 = ((bf16[32,16,768]{2,1,0:T(8,128)(2,1)}), bf16[32,16,768]{2,1,0:T(8,128)(2,1)S(1)}, u32[]{:S(2)}, u32[]{:S(2)}) async-start(bf16[32,16,768]{2,1,0:T(8,128)(2,1)} %bitcast.36), calls=%async_computation.4 | async-start | bytes 1572864 | tf_op jit(solution)/shard_map/all_to_all | solution.py:462
  243.9 17.6 %all-to-all-done.4 = bf16[32,16,768]{2,1,0:T(8,128)(2,1)S(1)} async-done(((bf16[32,16,768]{2,1,0:T(8,128)(2,1)}), bf16[32,16,768]{2,1,0:T(8,128)(2,1)S(1)}, u32[]{:S(2)}, u32[]{:S(2)}) %all-to-all-start.4) | async-done | bytes 786464 | tf_op jit(solution)/shard_map/all_to_all | solution.py:462
  263.1 6.1 %all-to-all-start.5 = ((bf16[8,8,768]{2,1,0:T(8,128)(2,1)}), bf16[8,8,768]{2,1,0:T(8,128)(2,1)S(1)}, u32[]{:S(2)}, u32[]{:S(2)}) async-start(bf16[8,8,768]{2,1,0:T(8,128)(2,1)} %shard_map.125), calls=%async_computation.5 | async-start | bytes 196608 | tf_op jit(solution)/shard_map/all_to_all | solution.py:471
  (183 shorter events, 91.3 us)
Async XLA Ops:
  7.2 51.5 %all-gather.2.cloned.1.call-start = ((), (), s32[]{:S(2)}) async-start(), calls=%async_computation.6 | async-start | bytes 3538944 | tf_op jit(solution)/shard_map/all_gather | solution.py:325
  13.1 35.7 %collective-permute-start = (bf16[2,64,2048]{2,1,0:T(8,128)(2,1)}, bf16[2,64,2048]{2,1,0:T(8,128)(2,1)}, u32[]{:S(2)}, u32[]{:S(2)}) collective-permute-start(bf16[2,64,2048]{2,1,0:T(8,128)(2,1)} %get-tuple-element.60), channel_id=1, source_target_pairs={{0,1},{1,2},{2,3},{3,0},{4,5},{5,6},{6,7},{7,4},{8,9},{9,10},{10,1... | collective-permute-start | bytes 1572872 | tf_op jit(solution)/shard_map/ppermute | solution.py:22
  15.1 38.3 %collective-permute-start.1 = (bf16[2,64,2048]{2,1,0:T(8,128)(2,1)}, bf16[2,64,2048]{2,1,0:T(8,128)(2,1)}, u32[]{:S(2)}, u32[]{:S(2)}) collective-permute-start(bf16[2,64,2048]{2,1,0:T(8,128)(2,1)} %get-tuple-element.62), channel_id=1, source_target_pairs={{0,2},{1,3},{2,0},{3,1},{4,6},{5,7},{6,4},{7,5},{8,10},{9,11},{10,... | collective-permute-start | bytes 1572872 | tf_op jit(solution)/shard_map/ppermute | solution.py:22
  17.6 35.9 %collective-permute-start.2 = (bf16[2,64,2048]{2,1,0:T(8,128)(2,1)S(1)}, bf16[2,64,2048]{2,1,0:T(8,128)(2,1)}, u32[]{:S(2)}, u32[]{:S(2)}) collective-permute-start(bf16[2,64,2048]{2,1,0:T(8,128)(2,1)S(1)} %get-tuple-element.63), channel_id=1, source_target_pairs={{0,3},{1,0},{2,1},{3,2},{4,7},{5,4},{6,5},{7,6},{8,11},{9,8},{10,9... | collective-permute-start | bytes 1572872 | tf_op jit(solution)/shard_map/ppermute | solution.py:22
  23.4 24.6 %all-to-all-start = ((f32[8,2,256]{2,1,0:T(2,128)}), f32[8,2,256]{2,1,0:T(2,128)S(1)}, u32[]{:S(2)}, u32[]{:S(2)}) async-start(f32[8,2,256]{2,1,0:T(2,128)} %copy.81), calls=%async_computation | async-start | bytes 32768 | tf_op jit(solution)/shard_map/all_to_all | solution.py:347
  31.6 35.2 %collective-permute-start.3 = (bf16[288,1536]{1,0:T(8,128)(2,1)}, bf16[288,1536]{1,0:T(8,128)(2,1)S(1)}, u32[]{:S(2)}, u32[]{:S(2)}) collective-permute-start(bf16[288,1536]{1,0:T(8,128)(2,1)} %get-tuple-element.72), channel_id=1, source_target_pairs={{0,64},{64,128},{128,192},{192,0},{1,65},{65,129},{129,193},{193,1... | collective-permute-start | bytes 2654216 | tf_op jit(solution)/shard_map/ppermute | solution.py:22
  32.9 39.8 %collective-permute-start.4 = (bf16[288,1536]{1,0:T(8,128)(2,1)}, bf16[288,1536]{1,0:T(8,128)(2,1)}, u32[]{:S(2)}, u32[]{:S(2)}) collective-permute-start(bf16[288,1536]{1,0:T(8,128)(2,1)} %get-tuple-element.73), channel_id=1, source_target_pairs={{0,128},{64,192},{128,0},{192,64},{1,129},{65,193},{129,1},{193,65... | collective-permute-start | bytes 2654216 | tf_op jit(solution)/shard_map/ppermute | solution.py:22
  48.8 23.9 %collective-permute-start.5 = (bf16[288,1536]{1,0:T(8,128)(2,1)}, bf16[288,1536]{1,0:T(8,128)(2,1)}, u32[]{:S(2)}, u32[]{:S(2)}) collective-permute-start(bf16[288,1536]{1,0:T(8,128)(2,1)} %get-tuple-element.74), channel_id=1, source_target_pairs={{0,192},{64,0},{128,64},{192,128},{1,193},{65,1},{129,65},{193,129... | collective-permute-start | bytes 2654216 | tf_op jit(solution)/shard_map/ppermute | solution.py:22
  58.6 20.5 %all-to-all-start.1 = ((bf16[8,256,128]{2,1,0:T(8,128)(2,1)}), bf16[8,256,128]{2,1,0:T(8,128)(2,1)S(1)}, u32[]{:S(2)}, u32[]{:S(2)}) async-start(bf16[8,256,128]{2,1,0:T(8,128)(2,1)} %shard_map.114), calls=%async_computation.1 | async-start | bytes 1048576 | tf_op jit(solution)/shard_map/all_to_all | solution.py:377
  65.4 10.9 %collective-permute-start.7 = (bf16[64,2048]{1,0:T(8,128)(2,1)S(1)}, bf16[64,2048]{1,0:T(8,128)(2,1)}, u32[]{:S(2)}, u32[]{:S(2)}) collective-permute-start(bf16[64,2048]{1,0:T(8,128)(2,1)S(1)} %copy-done.20), channel_id=1, source_target_pairs={{0,2},{1,3},{2,0},{3,1},{4,6},{5,7},{6,4},{7,5},{8,10},{9,11},{10,... | collective-permute-start | bytes 786440 | tf_op jit(solution)/shard_map/ppermute | solution.py:22
  66.7 11.8 %collective-permute-start.8 = (bf16[64,2048]{1,0:T(8,128)(2,1)S(1)}, bf16[64,2048]{1,0:T(8,128)(2,1)}, u32[]{:S(2)}, u32[]{:S(2)}) collective-permute-start(bf16[64,2048]{1,0:T(8,128)(2,1)S(1)} %copy-done.18), channel_id=1, source_target_pairs={{0,3},{1,0},{2,1},{3,2},{4,7},{5,4},{6,5},{7,6},{8,11},{9,8},{10,9... | collective-permute-start | bytes 786440 | tf_op jit(solution)/shard_map/ppermute | solution.py:22
  95.4 22.8 %all-to-all-start.2 = ((bf16[8,256,128]{2,1,0:T(8,128)(2,1)}), bf16[8,256,128]{2,1,0:T(8,128)(2,1)}, u32[]{:S(2)}, u32[]{:S(2)}) async-start(bf16[8,256,128]{2,1,0:T(8,128)(2,1)} %shard_map.118), calls=%async_computation.2 | async-start | bytes 1048576 | tf_op jit(solution)/shard_map/all_to_all | solution.py:399
  100.1 23.6 %collective-permute-start.16 = (bf16[288,1536]{1,0:T(8,128)(2,1)}, bf16[288,1536]{1,0:T(8,128)(2,1)}, u32[]{:S(2)}, u32[]{:S(2)}) collective-permute-start(bf16[288,1536]{1,0:T(8,128)(2,1)} %get-tuple-element.89), channel_id=1, source_target_pairs={{0,128},{64,192},{128,0},{192,64},{1,129},{65,193},{129,1},{193,65... | collective-permute-start | bytes 2654216 | tf_op jit(solution)/shard_map/ppermute | solution.py:22
  123.8 10.7 %collective-permute-start.19 = (bf16[32,2176]{1,0:T(8,128)(2,1)S(1)}, bf16[32,2176]{1,0:T(8,128)(2,1)S(1)}, u32[]{:S(2)}, u32[]{:S(2)}) collective-permute-start(bf16[32,2176]{1,0:T(8,128)(2,1)S(1)} %get-tuple-element.90), channel_id=1, source_target_pairs={{0,192},{64,0},{128,64},{192,128},{1,193},{65,1},{129,65},{193,129... | collective-permute-start | bytes 417800 | tf_op jit(solution)/shard_map/ppermute | solution.py:22
  151.7 26.7 %all-to-all-start.3 = ((bf16[32,16,768]{2,1,0:T(8,128)(2,1)}), bf16[32,16,768]{2,1,0:T(8,128)(2,1)S(1)}, u32[]{:S(2)}, u32[]{:S(2)}) async-start(bf16[32,16,768]{2,1,0:T(8,128)(2,1)} %shard_map.122), calls=%async_computation.3 | async-start | bytes 1572864 | tf_op jit(solution)/shard_map/all_to_all | solution.py:437
  157.0 21.4 %collective-permute-start.24 = (bf16[288,1536]{1,0:T(8,128)(2,1)}, bf16[288,1536]{1,0:T(8,128)(2,1)}, u32[]{:S(2)}, u32[]{:S(2)}) collective-permute-start(bf16[288,1536]{1,0:T(8,128)(2,1)} %get-tuple-element.96), channel_id=1, source_target_pairs={{0,64},{64,128},{128,192},{192,0},{1,65},{65,129},{129,193},{193,1... | collective-permute-start | bytes 2654216 | tf_op jit(solution)/shard_map/ppermute | solution.py:22
  157.1 21.3 %collective-permute-start.25 = (bf16[288,1536]{1,0:T(8,128)(2,1)}, bf16[288,1536]{1,0:T(8,128)(2,1)}, u32[]{:S(2)}, u32[]{:S(2)}) collective-permute-start(bf16[288,1536]{1,0:T(8,128)(2,1)} %get-tuple-element.97), channel_id=1, source_target_pairs={{0,192},{64,0},{128,64},{192,128},{1,193},{65,1},{129,65},{193,129... | collective-permute-start | bytes 2654216 | tf_op jit(solution)/shard_map/ppermute | solution.py:22
  188.8 16.2 %collective-permute-start.29 = (bf16[288,512]{1,0:T(8,128)(2,1)S(1)}, bf16[288,512]{1,0:T(8,128)(2,1)S(1)}, u32[]{:S(2)}, u32[]{:S(2)}) collective-permute-start(bf16[288,512]{1,0:T(8,128)(2,1)S(1)} %get-tuple-element.106), channel_id=1, source_target_pairs={{0,64},{64,128},{128,192},{192,0},{1,65},{65,129},{129,193},{193,1... | collective-permute-start | bytes 884744 | tf_op jit(solution)/shard_map/ppermute | solution.py:22
  206.0 16.2 %collective-permute-start.30 = (bf16[288,512]{1,0:T(8,128)(2,1)S(1)}, bf16[288,512]{1,0:T(8,128)(2,1)S(1)}, u32[]{:S(2)}, u32[]{:S(2)}) collective-permute-start(bf16[288,512]{1,0:T(8,128)(2,1)S(1)} %multiply_convert_fusion.h0), channel_id=1, source_target_pairs={{0,64},{64,128},{128,192},{192,0},{1,65},{65,129},{129,193},{193,1... | collective-permute-start | bytes 884744 | tf_op jit(solution)/shard_map/ppermute | solution.py:22
  231.0 30.5 %all-to-all-start.4 = ((bf16[32,16,768]{2,1,0:T(8,128)(2,1)}), bf16[32,16,768]{2,1,0:T(8,128)(2,1)S(1)}, u32[]{:S(2)}, u32[]{:S(2)}) async-start(bf16[32,16,768]{2,1,0:T(8,128)(2,1)} %bitcast.36), calls=%async_computation.4 | async-start | bytes 1572864 | tf_op jit(solution)/shard_map/all_to_all | solution.py:462
  240.2 29.0 %collective-permute-start.13 = (bf16[64,2048]{1,0:T(8,128)(2,1)S(1)}, bf16[64,2048]{1,0:T(8,128)(2,1)S(1)}, u32[]{:S(2)}, u32[]{:S(2)}) collective-permute-start(bf16[64,2048]{1,0:T(8,128)(2,1)S(1)} %copy-done.16), channel_id=1, source_target_pairs={{0,3},{1,0},{2,1},{3,2},{4,7},{5,4},{6,5},{7,6},{8,11},{9,8},{10,9... | collective-permute-start | bytes 786440 | tf_op jit(solution)/shard_map/ppermute | solution.py:22
  242.7 26.4 %collective-permute-start.14 = (bf16[64,2048]{1,0:T(8,128)(2,1)S(1)}, bf16[64,2048]{1,0:T(8,128)(2,1)S(1)}, u32[]{:S(2)}, u32[]{:S(2)}) collective-permute-start(bf16[64,2048]{1,0:T(8,128)(2,1)S(1)} %copy-done.14), channel_id=1, source_target_pairs={{0,2},{1,3},{2,0},{3,1},{4,6},{5,7},{6,4},{7,5},{8,10},{9,11},{10,... | collective-permute-start | bytes 786440 | tf_op jit(solution)/shard_map/ppermute | solution.py:22
  243.3 25.9 %collective-permute-start.15 = (bf16[64,2048]{1,0:T(8,128)(2,1)S(1)}, bf16[64,2048]{1,0:T(8,128)(2,1)S(1)}, u32[]{:S(2)}, u32[]{:S(2)}) collective-permute-start(bf16[64,2048]{1,0:T(8,128)(2,1)S(1)} %copy-done.12), channel_id=1, source_target_pairs={{0,1},{1,2},{2,3},{3,0},{4,5},{5,6},{6,7},{7,4},{8,9},{9,10},{10,1... | collective-permute-start | bytes 786440 | tf_op jit(solution)/shard_map/ppermute | solution.py:22
  263.1 11.1 %all-to-all-start.5 = ((bf16[8,8,768]{2,1,0:T(8,128)(2,1)}), bf16[8,8,768]{2,1,0:T(8,128)(2,1)S(1)}, u32[]{:S(2)}, u32[]{:S(2)}) async-start(bf16[8,8,768]{2,1,0:T(8,128)(2,1)} %shard_map.125), calls=%async_computation.5 | async-start | bytes 196608 | tf_op jit(solution)/shard_map/all_to_all | solution.py:471
  (44 other events, 513.5 us)
Sparse Core Ops, SparseCore 0:
  9.8 48.8 all-gather.1

commit v3 on v2

--- a/solution.py
+++ b/solution.py
@@ -20,6 +20,10 @@
 def shifted(v, axis, by):
     n = lax.axis_size(axis)
     return lax.ppermute(v, axis, [(i, (i + by) % n) for i in range(n)])
+
+
+def in_hbm(a):
+    return pltpu.with_memory_space_constraint(a, pltpu.HBM)
 
 
 def kernel_call(body, outs, args, scalars=0, flops=0, steps=None, blocks=None):
@@ -37,7 +41,7 @@
     inputs = len(args) - scalars
     if steps is not None:
         args = [
-            pltpu.with_memory_space_constraint(a, pltpu.HBM)
+            in_hbm(a)
             if i >= scalars and a.dtype == bf16 and a.size >= 1 << 17
             else a
             for i, a in enumerate(args)
@@ -235,13 +239,12 @@
         out[...] = part.astype(bf16)
 
 
-def down_body(ids, h0, h1, h2, h3, w0, w1, w2, w3, keep, send):
-    width = keep.shape[1]
-    mine = pl.ds(pl.multiple_of(ids[2] * width, HEAD), width)
-    rest = pl.ds(pl.multiple_of((1 - ids[2]) * width, HEAD), width)
+def down_body(ids, h0, h1, h2, h3, w0, w1, w2, w3, out, *, other):
+    width = out.shape[1]
+    part = 1 - ids[2] if other else ids[2]
+    cols = pl.ds(pl.multiple_of(part * width, HEAD), width)
     hs, ws = (h0, h1, h2, h3), (w0, w1, w2, w3)
-    send[...] = sum(dot(h[...], w[:, rest], ((0,), (0,))) for h, w in zip(hs, ws)).astype(bf16)
-    keep[...] = sum(dot(h[...], w[:, mine], ((0,), (0,))) for h, w in zip(hs, ws))
+    out[...] = sum(dot(h[...], w[:, cols], ((0,), (0,))) for h, w in zip(hs, ws)).astype(out.dtype)
 
 
 def combine_body(ids, back, table, out):
@@ -319,7 +322,6 @@
     )
     kv_out = list(kv_out)
     kv = over_x(kv_out)
-    queries, kv[1] = lax.optimization_barrier((queries, kv[1]))
     q_out = kernel_call(pack_body, [struct((tokens, features), bf16)] * 4, (ids, queries), scalars=1)
 
     weight_out = lax.all_gather(out_proj, "z", axis=0, tiled=True)
@@ -334,7 +336,7 @@
         return [pieces[0]] + [shifted(pieces[d], "y", d) for d in range(1, 4)]
 
     up = sliced(up_weight[0].T)
-    kv[0], log_decay, *up = lax.optimization_barrier((kv_out[0], log_decay, *up))
+    kv[0], log_decay = lax.optimization_barrier((kv_out[0], log_decay))
     up = over_y(up)
 
     decay = log_decay.T.reshape(2 * n_z, length)
@@ -443,7 +445,7 @@
     parts = kernel_call(
         up_body,
         [struct((hidden_dev, arrived.shape[0]), bf16)] * 4,
-        (ids, arrived, shifted(arrived, "c", 1), *up),
+        (ids, arrived, shifted(arrived, "c", 1), *map(in_hbm, up)),
         scalars=1,
         flops=16 * arrived.size * hidden_dev,
     )
@@ -451,13 +453,17 @@
     hidden = jax.nn.silu(sum(p.astype(f32) for p in parts)).astype(bf16)
     mixed = [mixed[0]] + [shifted(mixed[d], "x", -d) for d in range(1, 4)]
     hiddens = [hidden] + [shifted(hidden, "y", d) for d in range(1, 4)]
-    keep, send = kernel_call(
-        down_body,
-        [struct(arrived.shape, f32), struct(arrived.shape, bf16)],
-        (ids, *hiddens, *down),
-        scalars=1,
-        flops=16 * arrived.size * hidden_dev,
-    )
+    def down_half(other, dtype):
+        return kernel_call(
+            lambda *refs: down_body(*refs, other=other),
+            [struct(arrived.shape, dtype)],
+            (ids, *hiddens, *down),
+            scalars=1,
+            flops=8 * arrived.size * hidden_dev,
+        )[0]
+
+    send = down_half(True, bf16)
+    keep = down_half(False, f32)
     result = (keep + shifted(send, "c", 1).astype(f32)).astype(bf16)
     back = lax.all_to_all(
         result.reshape(outgoing.shape), EP, 0, 0, tiled=True

time: 283 us -> 284 us (level)
  waiting for transfers between devices: 121 us -> 116 us
  local copies, waits for them, and re-layouts: 19.9 us -> 24.8 us
    ppermute x34, waiting for transfers between devices: 86.4 us -> 80.7 us  [shifted(): return lax.ppermute(v, axis, [(i, (i + by) % n) for i in range(n)])]
    unnamed x60 -> x64, local copies, waits for them, and re-layouts: 8.88 us -> 10.9 us
    pallas_call x13 -> x14, Pallas kernels: 34 us -> 35.1 us  [kernel_call(): pl.pallas_call(body, out_shape=tuple(outs), grid=() if steps is None else...]
  transfers between devices with their start and end apart: 41 -> 41, of which waited for: 27 -> 23; matrix products, arithmetic and copies ran while one was open for 4% -> 6% of each run, Pallas kernels for 7% -> 8%
where the time goes in v3:
time: 284 us; the launch traced here: 282 us
  waiting for transfers between devices  116 us (41%)
  starting transfers between devices  80.1 us (28%)
  Pallas kernels  35.1 us (12%)
  local copies, waits for them, and re-layouts  24.8 us (9%)
  between operations  22.1 us (8%)
  other arithmetic  2.98 us (1%)
    ppermute x34, waiting for transfers between devices, shifted(): return lax.ppermute(v, axis, [(i, (i + by) % n) for i in range(n)])  80.7 us
    ppermute x34, starting transfers between devices, shifted(): return lax.ppermute(v, axis, [(i, (i + by) % n) for i in range(n)])  42.3 us
    pallas_call x14, Pallas kernels, kernel_call(): pl.pallas_call(body, out_shape=tuple(outs), grid=() if steps is None else...  35.1 us
    all_to_all x1, waiting for transfers between devices, on_device(): lax.all_to_all(result.reshape(outgoing.shape), EP, 0, 0, tiled=True)  18.4 us
    all_to_all x1, waiting for transfers between devices, on_device(): prefix = lax.all_to_all(prefix, 'z', 0, 0, tiled=True)  11.8 us
    unnamed x64, local copies, waits for them, and re-layouts  10.9 us
    all_to_all x1, starting transfers between devices, on_device(): lax.all_to_all(result.reshape(outgoing.shape), EP, 0, 0, tiled=True)  9.23 us
    all_to_all x1, starting transfers between devices, on_device(): lax.all_to_all(rel_own.transpose(1, 0, 2), 'z', 0, 0, tiled=True)  9.01 us
  transfers between devices with their start and end apart: 41, of which 23 were waited for; matrix products, arithmetic and copies ran while one was open for 6% of the time, Pallas kernels for 8%

profile of v3, /device:TPU:1, one launch (start us, length us, event | category | flops | bytes accessed | tf_op | source)
XLA Modules:
  0.0 282.1 jit_solution(11800962794642597047)
XLA Ops:
  14.4 9.0 %all-to-all-start = ((f32[8,2,256]{2,1,0:T(2,128)}), f32[8,2,256]{2,1,0:T(2,128)S(1)}, u32[]{:S(2)}, u32[]{:S(2)}) async-start(f32[8,2,256]{2,1,0:T(2,128)} %copy.81), calls=%async_computation | async-start | bytes 32768 | tf_op jit(solution)/shard_map/all_to_all | solution.py:349
  28.2 3.8 %dynamic-slice_bitcast_fusion = (bf16[288,1536]{1,0:T(8,128)(2,1)}, bf16[288,1536]{1,0:T(8,128)(2,1)}, bf16[288,1536]{1,0:T(8,128)(2,1)}, bf16[288,1536]{1,0:T(8,128)(2,1)}) fusion(bf16[1,6144,288]{1,2,0:T(8,128)(2,1)} %param.18, s32[]{:T(128)S(6)} %select_n.113, s32[]{:T(128)S(6)} %select_n.109, s32[]{:T(128)S(6)} %select_n.107, s32[]{:T(128)S(6)} %select_n.111), kind=kLoop, calls=%fused_computation.1 | loop fusion | bytes 7077904 | tf_op jit(solution)/shard_map/dynamic_slice | solution.py:332
  35.5 3.7 %dynamic-slice_bitcast_fusion.4 = (bf16[288,1536]{1,0:T(8,128)(2,1)}, bf16[288,1536]{1,0:T(8,128)(2,1)}, bf16[288,1536]{1,0:T(8,128)(2,1)S(1)}, bf16[288,1536]{1,0:T(8,128)(2,1)}) fusion(bf16[1,288,6144]{2,1,0:T(8,128)(2,1)} %param.19, s32[]{:T(128)S(6)} %select_n.113, s32[]{:T(128)S(6)} %select_n.109, s32[]{:T(128)S(6)} %select_n.107, s32[]{:T(128)S(6)} %select_n.111), kind=kLoop, calls=%fused_computation.5 | loop fusion | bytes 7077904 | tf_op jit(solution)/shard_map/dynamic_slice | solution.py:332
  52.8 4.5 %shard_map.114 = bf16[8,256,128]{2,1,0:T(8,128)(2,1)} custom-call(bf16[2,64,2048]{2,1,0:T(8,128)(2,1)} %copy-done.1, bf16[2,64,2048]{2,1,0:T(8,128)(2,1)} %collective-permute-done.kv1, bf16[2,64,2048]{2,1,0:T(8,128)(2,1)} %collective-permute-done.1.kv2, bf16[2,64,2048]{2,1,0:T(8,128)(2,1)} %collective-permute-done.2.kv3, f32[4,256,4]{2,1,0:T(8,128)S(1)} %bitcast.62, ...), custom_call_target="tpu_custom_call" | custom-call | flops 134217728 | bytes 2637888 | tf_op jit(solution)/shard_map/pallas_call | solution.py:49
  58.5 5.6 %all-to-all-start.1 = ((bf16[8,256,128]{2,1,0:T(8,128)(2,1)}), bf16[8,256,128]{2,1,0:T(8,128)(2,1)S(1)}, u32[]{:S(2)}, u32[]{:S(2)}) async-start(bf16[8,256,128]{2,1,0:T(8,128)(2,1)} %shard_map.114), calls=%async_computation.1 | async-start | bytes 1048576 | tf_op jit(solution)/shard_map/all_to_all | solution.py:379
  68.3 6.4 %collective-permute-done.4.w2 = bf16[288,1536]{1,0:T(8,128)(2,1)} collective-permute-done((bf16[288,1536]{1,0:T(8,128)(2,1)}, bf16[288,1536]{1,0:T(8,128)(2,1)}, u32[]{:S(2)}, u32[]{:S(2)}) %collective-permute-start.4) | collective-permute-done | bytes 884768 | tf_op jit(solution)/shard_map/ppermute | solution.py:22
  86.9 6.2 %collective-permute-start.12 = (bf16[1088,128]{1,0:T(8,128)(2,1)S(1)}, bf16[1088,128]{1,0:T(8,128)(2,1)S(1)}, u32[]{:S(2)}, u32[]{:S(2)}) collective-permute-start(bf16[1088,128]{1,0:T(8,128)(2,1)S(1)} %pad_maximum_fusion.g0), channel_id=1, source_target_pairs={{0,32},{32,0},{1,33},{33,1},{2,34},{34,2},{3,35},{35,3},{4,36},{36... | collective-permute-start | bytes 835592 | tf_op jit(solution)/shard_map/ppermute | solution.py:22
  97.3 4.7 %all-to-all-start.2 = ((bf16[8,256,128]{2,1,0:T(8,128)(2,1)}), bf16[8,256,128]{2,1,0:T(8,128)(2,1)}, u32[]{:S(2)}, u32[]{:S(2)}) async-start(bf16[8,256,128]{2,1,0:T(8,128)(2,1)} %shard_map.118), calls=%async_computation.2 | async-start | bytes 1048576 | tf_op jit(solution)/shard_map/all_to_all | solution.py:401
  103.7 4.6 %shard_map.116.inside = f32[256,2048]{1,0:T(8,128)S(1)} custom-call(s32[3]{0:T(128)S(1)} %copy-done.12, bf16[64,2048]{1,0:T(8,128)(2,1)} %copy-done.3, bf16[64,2048]{1,0:T(8,128)(2,1)} %copy-done.25, bf16[64,2048]{1,0:T(8,128)(2,1)} %copy-done.26, bf16[64,2048]{1,0:T(8,128)(2,1)} %collective-permute-done.8.q3, bf16[2,64,2048]{2,1,0:T(8,128)(2,1)} %copy-done.1, ...), custom_call_target="tpu_custom_call" | custom-call | flops 536870912 | bytes 5275660 | tf_op jit(solution)/shard_map/pallas_call | solution.py:49
  108.3 11.8 %all-to-all-done.2.prefix = bf16[8,256,128]{2,1,0:T(8,128)(2,1)} async-done(((bf16[8,256,128]{2,1,0:T(8,128)(2,1)}), bf16[8,256,128]{2,1,0:T(8,128)(2,1)}, u32[]{:S(2)}, u32[]{:S(2)}) %all-to-all-start.2) | async-done | bytes 524320 | tf_op jit(solution)/shard_map/all_to_all | solution.py:401
  120.8 5.5 %shard_map.119 = (bf16[64,2048]{1,0:T(8,128)(2,1)S(1)}, bf16[64,2048]{1,0:T(8,128)(2,1)S(1)}, bf16[64,2048]{1,0:T(8,128)(2,1)S(1)}, bf16[64,2048]{1,0:T(8,128)(2...) custom-call(f32[256,2048]{1,0:T(8,128)S(1)} %shard_map.116.inside, bf16[64,2048]{1,0:T(8,128)(2,1)} %copy-done.3, ...), custom_call_target="tpu_custom_call" | custom-call | flops 134217728 | bytes 4898816 | tf_op jit(solution)/shard_map/pallas_call | solution.py:49
  127.9 8.7 %collective-permute-done.17 = bf16[32,2176]{1,0:T(8,128)(2,1)S(1)} collective-permute-done((bf16[32,2176]{1,0:T(8,128)(2,1)S(1)}, bf16[32,2176]{1,0:T(8,128)(2,1)S(1)}, u32[]{:S(2)}, u32[]{:S(2)}) %collective-permute-start.17) | collective-permute-done | bytes 139296 | tf_op jit(solution)/shard_map/ppermute | solution.py:22
  145.1 4.0 %collective-permute-done.21.refs_1_ = bf16[64,896]{1,0:T(8,128)(2,1)S(1)} collective-permute-done((bf16[64,896]{1,0:T(8,128)(2,1)S(1)}, bf16[64,896]{1,0:T(8,128)(2,1)S(1)}, u32[]{:S(2)}, u32[]{:S(2)}) %collective-permute-start.21) | collective-permute-done | bytes 114720 | tf_op jit(solution)/shard_map/ppermute | solution.py:22
  154.1 4.6 %all-to-all-start.3 = ((bf16[32,16,768]{2,1,0:T(8,128)(2,1)}), bf16[32,16,768]{2,1,0:T(8,128)(2,1)S(1)}, u32[]{:S(2)}, u32[]{:S(2)}) async-start(bf16[32,16,768]{2,1,0:T(8,128)(2,1)} %shard_map.122), calls=%async_computation.3 | async-start | bytes 1572864 | tf_op jit(solution)/shard_map/all_to_all | solution.py:439
  163.8 16.2 %collective-permute-done.24.refs_6_ = bf16[288,1536]{1,0:T(8,128)(2,1)S(1)} collective-permute-done((bf16[288,1536]{1,0:T(8,128)(2,1)}, bf16[288,1536]{1,0:T(8,128)(2,1)S(1)}, u32[]{:S(2)}, u32[]{:S(2)}) %collective-permute-start.24) | collective-permute-done | bytes 884768 | tf_op jit(solution)/shard_map/ppermute | solution.py:22
  184.5 4.0 %shard_map.123 = (bf16[288,512]{1,0:T(8,128)(2,1)S(1)}, bf16[288,512]{1,0:T(8,128)(2,1)S(1)}, bf16[288,512]{1,0:T(8,128)(2,1)S(1)}, bf16[288,512]{1,0:T(8,128)(2,1)S(1)}) custom-call(s32[3]{0:T(128)S(1)} %copy-done.13, bf16[512,768]{1,0:T(8,128)(2,1)S(1)} %bitcast.68, bf16[512,768]{1,0:T(8,128)(2,1)S(1)} %collective-permute-done.26.other, ...), custom_call_target="tpu_custom_call" | custom-call | flops 1811939328 | bytes 6291468 | tf_op jit(solution)/shard_map/pallas_call | solution.py:49
  191.6 6.0 %collective-permute-done.27 = bf16[288,512]{1,0:T(8,128)(2,1)S(1)} collective-permute-done((bf16[288,512]{1,0:T(8,128)(2,1)S(1)}, bf16[288,512]{1,0:T(8,128)(2,1)S(1)}, u32[]{:S(2)}, u32[]{:S(2)}) %collective-permute-start.27) | collective-permute-done | bytes 294944 | tf_op jit(solution)/shard_map/ppermute | solution.py:22
  200.4 6.7 %collective-permute-done.29 = bf16[288,512]{1,0:T(8,128)(2,1)S(1)} collective-permute-done((bf16[288,512]{1,0:T(8,128)(2,1)S(1)}, bf16[288,512]{1,0:T(8,128)(2,1)S(1)}, u32[]{:S(2)}, u32[]{:S(2)}) %collective-permute-start.29) | collective-permute-done | bytes 294944 | tf_op jit(solution)/shard_map/ppermute | solution.py:22
  208.9 6.3 %collective-permute-done.32.refs_4_ = bf16[288,512]{1,0:T(8,128)(2,1)S(1)} collective-permute-done((bf16[288,512]{1,0:T(8,128)(2,1)S(1)}, bf16[288,512]{1,0:T(8,128)(2,1)S(1)}, u32[]{:S(2)}, u32[]{:S(2)}) %collective-permute-start.32) | collective-permute-done | bytes 294944 | tf_op jit(solution)/shard_map/ppermute | solution.py:22
  216.0 8.3 %collective-permute-done.30.refs_2_ = bf16[288,512]{1,0:T(8,128)(2,1)S(1)} collective-permute-done((bf16[288,512]{1,0:T(8,128)(2,1)S(1)}, bf16[288,512]{1,0:T(8,128)(2,1)S(1)}, u32[]{:S(2)}, u32[]{:S(2)}) %collective-permute-start.30) | collective-permute-done | bytes 294944 | tf_op jit(solution)/shard_map/ppermute | solution.py:22
  224.3 3.0 %shard_map.125 = bf16[512,768]{1,0:T(8,128)(2,1)S(1)} custom-call(s32[3]{0:T(128)S(1)} %copy-done.13, bf16[288,512]{1,0:T(8,128)(2,1)S(1)} %multiply_convert_fusion.refs_1_, bf16[288,512]{1,0:T(8,128)(2,1)S(1)} %collective-permute-done.30.refs_2_, bf16[288,512]{1,0:T(8,128)(2,1)S(1)} %collective-permute-done.31.refs_3_, ...), custom_call_target="tpu_custom_call" | custom-call | flops 905969664 | bytes 5505036 | tf_op jit(solution)/shard_map/pallas_call | solution.py:49
  232.0 9.2 %all-to-all-start.4 = ((bf16[32,16,768]{2,1,0:T(8,128)(2,1)}), bf16[32,16,768]{2,1,0:T(8,128)(2,1)S(1)}, u32[]{:S(2)}, u32[]{:S(2)}) async-start(bf16[32,16,768]{2,1,0:T(8,128)(2,1)} %bitcast.36), calls=%async_computation.4 | async-start | bytes 1572864 | tf_op jit(solution)/shard_map/all_to_all | solution.py:468
  244.9 18.4 %all-to-all-done.4 = bf16[32,16,768]{2,1,0:T(8,128)(2,1)S(1)} async-done(((bf16[32,16,768]{2,1,0:T(8,128)(2,1)}), bf16[32,16,768]{2,1,0:T(8,128)(2,1)S(1)}, u32[]{:S(2)}, u32[]{:S(2)}) %all-to-all-start.4) | async-done | bytes 786464 | tf_op jit(solution)/shard_map/all_to_all | solution.py:468
  265.0 4.6 %all-to-all-start.5 = ((bf16[8,8,768]{2,1,0:T(8,128)(2,1)}), bf16[8,8,768]{2,1,0:T(8,128)(2,1)S(1)}, u32[]{:S(2)}, u32[]{:S(2)}) async-start(bf16[8,8,768]{2,1,0:T(8,128)(2,1)} %shard_map.126), calls=%async_computation.5 | async-start | bytes 196608 | tf_op jit(solution)/shard_map/all_to_all | solution.py:477
  (188 shorter events, 94.1 us)
Async XLA Ops:
  7.2 51.3 %all-gather.2.cloned.1.call-start = ((), (), s32[]{:S(2)}) async-start(), calls=%async_computation.6 | async-start | bytes 3538944 | tf_op jit(solution)/shard_map/all_gather | solution.py:327
  14.4 35.8 %all-to-all-start = ((f32[8,2,256]{2,1,0:T(2,128)}), f32[8,2,256]{2,1,0:T(2,128)S(1)}, u32[]{:S(2)}, u32[]{:S(2)}) async-start(f32[8,2,256]{2,1,0:T(2,128)} %copy.81), calls=%async_computation | async-start | bytes 32768 | tf_op jit(solution)/shard_map/all_to_all | solution.py:349
  23.4 27.6 %collective-permute-start = (bf16[2,64,2048]{2,1,0:T(8,128)(2,1)}, bf16[2,64,2048]{2,1,0:T(8,128)(2,1)}, u32[]{:S(2)}, u32[]{:S(2)}) collective-permute-start(bf16[2,64,2048]{2,1,0:T(8,128)(2,1)} %get-tuple-element.52), channel_id=1, source_target_pairs={{0,1},{1,2},{2,3},{3,0},{4,5},{5,6},{6,7},{7,4},{8,9},{9,10},{10,1... | collective-permute-start | bytes 1572872 | tf_op jit(solution)/shard_map/ppermute | solution.py:22
  24.6 28.1 %collective-permute-start.1 = (bf16[2,64,2048]{2,1,0:T(8,128)(2,1)S(1)}, bf16[2,64,2048]{2,1,0:T(8,128)(2,1)}, u32[]{:S(2)}, u32[]{:S(2)}) collective-permute-start(bf16[2,64,2048]{2,1,0:T(8,128)(2,1)S(1)} %get-tuple-element.53), channel_id=1, source_target_pairs={{0,2},{1,3},{2,0},{3,1},{4,6},{5,7},{6,4},{7,5},{8,10},{9,11},{10,... | collective-permute-start | bytes 1572872 | tf_op jit(solution)/shard_map/ppermute | solution.py:22
  27.1 25.7 %collective-permute-start.2 = (bf16[2,64,2048]{2,1,0:T(8,128)(2,1)S(1)}, bf16[2,64,2048]{2,1,0:T(8,128)(2,1)}, u32[]{:S(2)}, u32[]{:S(2)}) collective-permute-start(bf16[2,64,2048]{2,1,0:T(8,128)(2,1)S(1)} %get-tuple-element.54), channel_id=1, source_target_pairs={{0,3},{1,0},{2,1},{3,2},{4,7},{5,4},{6,5},{7,6},{8,11},{9,8},{10,9... | collective-permute-start | bytes 1572872 | tf_op jit(solution)/shard_map/ppermute | solution.py:22
  32.1 34.5 %collective-permute-start.5 = (bf16[288,1536]{1,0:T(8,128)(2,1)}, bf16[288,1536]{1,0:T(8,128)(2,1)}, u32[]{:S(2)}, u32[]{:S(2)}) collective-permute-start(bf16[288,1536]{1,0:T(8,128)(2,1)} %get-tuple-element.100), channel_id=1, source_target_pairs={{0,192},{64,0},{128,64},{192,128},{1,193},{65,1},{129,65},{193,129... | collective-permute-start | bytes 2654216 | tf_op jit(solution)/shard_map/ppermute | solution.py:22
  34.8 33.5 %collective-permute-start.3 = (bf16[288,1536]{1,0:T(8,128)(2,1)}, bf16[288,1536]{1,0:T(8,128)(2,1)}, u32[]{:S(2)}, u32[]{:S(2)}) collective-permute-start(bf16[288,1536]{1,0:T(8,128)(2,1)} %get-tuple-element.101), channel_id=1, source_target_pairs={{0,64},{64,128},{128,192},{192,0},{1,65},{65,129},{129,193},{193,1... | collective-permute-start | bytes 2654216 | tf_op jit(solution)/shard_map/ppermute | solution.py:22
  51.0 23.7 %collective-permute-start.4 = (bf16[288,1536]{1,0:T(8,128)(2,1)}, bf16[288,1536]{1,0:T(8,128)(2,1)}, u32[]{:S(2)}, u32[]{:S(2)}) collective-permute-start(bf16[288,1536]{1,0:T(8,128)(2,1)} %get-tuple-element.103), channel_id=1, source_target_pairs={{0,128},{64,192},{128,0},{192,64},{1,129},{65,193},{129,1},{193,65... | collective-permute-start | bytes 2654216 | tf_op jit(solution)/shard_map/ppermute | solution.py:22
  58.5 19.9 %all-to-all-start.1 = ((bf16[8,256,128]{2,1,0:T(8,128)(2,1)}), bf16[8,256,128]{2,1,0:T(8,128)(2,1)S(1)}, u32[]{:S(2)}, u32[]{:S(2)}) async-start(bf16[8,256,128]{2,1,0:T(8,128)(2,1)} %shard_map.114), calls=%async_computation.1 | async-start | bytes 1048576 | tf_op jit(solution)/shard_map/all_to_all | solution.py:379
  64.2 10.5 %collective-permute-start.6 = (bf16[64,2048]{1,0:T(8,128)(2,1)S(1)}, bf16[64,2048]{1,0:T(8,128)(2,1)S(1)}, u32[]{:S(2)}, u32[]{:S(2)}) collective-permute-start(bf16[64,2048]{1,0:T(8,128)(2,1)S(1)} %copy-done.24), channel_id=1, source_target_pairs={{0,1},{1,2},{2,3},{3,0},{4,5},{5,6},{6,7},{7,4},{8,9},{9,10},{10,1... | collective-permute-start | bytes 786440 | tf_op jit(solution)/shard_map/ppermute | solution.py:22
  64.6 12.0 %collective-permute-start.7 = (bf16[64,2048]{1,0:T(8,128)(2,1)S(1)}, bf16[64,2048]{1,0:T(8,128)(2,1)S(1)}, u32[]{:S(2)}, u32[]{:S(2)}) collective-permute-start(bf16[64,2048]{1,0:T(8,128)(2,1)S(1)} %copy-done.22), channel_id=1, source_target_pairs={{0,2},{1,3},{2,0},{3,1},{4,6},{5,7},{6,4},{7,5},{8,10},{9,11},{10,... | collective-permute-start | bytes 786440 | tf_op jit(solution)/shard_map/ppermute | solution.py:22
  66.6 11.4 %collective-permute-start.8 = (bf16[64,2048]{1,0:T(8,128)(2,1)S(1)}, bf16[64,2048]{1,0:T(8,128)(2,1)}, u32[]{:S(2)}, u32[]{:S(2)}) collective-permute-start(bf16[64,2048]{1,0:T(8,128)(2,1)S(1)} %get-tuple-element.64), channel_id=1, source_target_pairs={{0,3},{1,0},{2,1},{3,2},{4,7},{5,4},{6,5},{7,6},{8,11},{9,8},{10,9... | collective-permute-start | bytes 786440 | tf_op jit(solution)/shard_map/ppermute | solution.py:22
  97.3 22.8 %all-to-all-start.2 = ((bf16[8,256,128]{2,1,0:T(8,128)(2,1)}), bf16[8,256,128]{2,1,0:T(8,128)(2,1)}, u32[]{:S(2)}, u32[]{:S(2)}) async-start(bf16[8,256,128]{2,1,0:T(8,128)(2,1)} %shard_map.118), calls=%async_computation.2 | async-start | bytes 1048576 | tf_op jit(solution)/shard_map/all_to_all | solution.py:401
  102.0 24.3 %collective-permute-start.16 = (bf16[288,1536]{1,0:T(8,128)(2,1)}, bf16[288,1536]{1,0:T(8,128)(2,1)}, u32[]{:S(2)}, u32[]{:S(2)}) collective-permute-start(bf16[288,1536]{1,0:T(8,128)(2,1)} %get-tuple-element.75), channel_id=1, source_target_pairs={{0,128},{64,192},{128,0},{192,64},{1,129},{65,193},{129,1},{193,65... | collective-permute-start | bytes 2654216 | tf_op jit(solution)/shard_map/ppermute | solution.py:22
  126.3 10.3 %collective-permute-start.19 = (bf16[32,2176]{1,0:T(8,128)(2,1)S(1)}, bf16[32,2176]{1,0:T(8,128)(2,1)S(1)}, u32[]{:S(2)}, u32[]{:S(2)}) collective-permute-start(bf16[32,2176]{1,0:T(8,128)(2,1)S(1)} %get-tuple-element.76), channel_id=1, source_target_pairs={{0,192},{64,0},{128,64},{192,128},{1,193},{65,1},{129,65},{193,129... | collective-permute-start | bytes 417800 | tf_op jit(solution)/shard_map/ppermute | solution.py:22
  154.1 25.8 %all-to-all-start.3 = ((bf16[32,16,768]{2,1,0:T(8,128)(2,1)}), bf16[32,16,768]{2,1,0:T(8,128)(2,1)S(1)}, u32[]{:S(2)}, u32[]{:S(2)}) async-start(bf16[32,16,768]{2,1,0:T(8,128)(2,1)} %shard_map.122), calls=%async_computation.3 | async-start | bytes 1572864 | tf_op jit(solution)/shard_map/all_to_all | solution.py:439
  158.7 21.3 %collective-permute-start.24 = (bf16[288,1536]{1,0:T(8,128)(2,1)}, bf16[288,1536]{1,0:T(8,128)(2,1)S(1)}, u32[]{:S(2)}, u32[]{:S(2)}) collective-permute-start(bf16[288,1536]{1,0:T(8,128)(2,1)} %get-tuple-element.82), channel_id=1, source_target_pairs={{0,64},{64,128},{128,192},{192,0},{1,65},{65,129},{129,193},{193,1... | collective-permute-start | bytes 2654216 | tf_op jit(solution)/shard_map/ppermute | solution.py:22
  158.8 21.2 %collective-permute-start.25 = (bf16[288,1536]{1,0:T(8,128)(2,1)}, bf16[288,1536]{1,0:T(8,128)(2,1)S(1)}, u32[]{:S(2)}, u32[]{:S(2)}) collective-permute-start(bf16[288,1536]{1,0:T(8,128)(2,1)} %get-tuple-element.83), channel_id=1, source_target_pairs={{0,192},{64,0},{128,64},{192,128},{1,193},{65,1},{129,65},{193,129... | collective-permute-start | bytes 2654216 | tf_op jit(solution)/shard_map/ppermute | solution.py:22
  191.0 16.2 %collective-permute-start.29 = (bf16[288,512]{1,0:T(8,128)(2,1)S(1)}, bf16[288,512]{1,0:T(8,128)(2,1)S(1)}, u32[]{:S(2)}, u32[]{:S(2)}) collective-permute-start(bf16[288,512]{1,0:T(8,128)(2,1)S(1)} %get-tuple-element.92), channel_id=1, source_target_pairs={{0,64},{64,128},{128,192},{192,0},{1,65},{65,129},{129,193},{193,1... | collective-permute-start | bytes 884744 | tf_op jit(solution)/shard_map/ppermute | solution.py:22
  208.1 16.2 %collective-permute-start.30 = (bf16[288,512]{1,0:T(8,128)(2,1)S(1)}, bf16[288,512]{1,0:T(8,128)(2,1)S(1)}, u32[]{:S(2)}, u32[]{:S(2)}) collective-permute-start(bf16[288,512]{1,0:T(8,128)(2,1)S(1)} %multiply_convert_fusion.refs_1_), channel_id=1, source_target_pairs={{0,64},{64,128},{128,192},{192,0},{1,65},{65,129},{129,193},{193,1... | collective-permute-start | bytes 884744 | tf_op jit(solution)/shard_map/ppermute | solution.py:22
  232.0 31.3 %all-to-all-start.4 = ((bf16[32,16,768]{2,1,0:T(8,128)(2,1)}), bf16[32,16,768]{2,1,0:T(8,128)(2,1)S(1)}, u32[]{:S(2)}, u32[]{:S(2)}) async-start(bf16[32,16,768]{2,1,0:T(8,128)(2,1)} %bitcast.36), calls=%async_computation.4 | async-start | bytes 1572864 | tf_op jit(solution)/shard_map/all_to_all | solution.py:468
  241.3 28.4 %collective-permute-start.13 = (bf16[64,2048]{1,0:T(8,128)(2,1)S(1)}, bf16[64,2048]{1,0:T(8,128)(2,1)S(1)}, u32[]{:S(2)}, u32[]{:S(2)}) collective-permute-start(bf16[64,2048]{1,0:T(8,128)(2,1)S(1)} %copy-done.20), channel_id=1, source_target_pairs={{0,3},{1,0},{2,1},{3,2},{4,7},{5,4},{6,5},{7,6},{8,11},{9,8},{10,9... | collective-permute-start | bytes 786440 | tf_op jit(solution)/shard_map/ppermute | solution.py:22
  243.8 25.8 %collective-permute-start.14 = (bf16[64,2048]{1,0:T(8,128)(2,1)S(1)}, bf16[64,2048]{1,0:T(8,128)(2,1)S(1)}, u32[]{:S(2)}, u32[]{:S(2)}) collective-permute-start(bf16[64,2048]{1,0:T(8,128)(2,1)S(1)} %copy-done.18), channel_id=1, source_target_pairs={{0,2},{1,3},{2,0},{3,1},{4,6},{5,7},{6,4},{7,5},{8,10},{9,11},{10,... | collective-permute-start | bytes 786440 | tf_op jit(solution)/shard_map/ppermute | solution.py:22
  244.4 25.3 %collective-permute-start.15 = (bf16[64,2048]{1,0:T(8,128)(2,1)S(1)}, bf16[64,2048]{1,0:T(8,128)(2,1)S(1)}, u32[]{:S(2)}, u32[]{:S(2)}) collective-permute-start(bf16[64,2048]{1,0:T(8,128)(2,1)S(1)} %copy-done.16), channel_id=1, source_target_pairs={{0,1},{1,2},{2,3},{3,0},{4,5},{5,6},{6,7},{7,4},{8,9},{9,10},{10,1... | collective-permute-start | bytes 786440 | tf_op jit(solution)/shard_map/ppermute | solution.py:22
  (46 other events, 532.9 us)
Sparse Core Ops, SparseCore 0:
  9.8 48.6 all-gather.1
